TPU v7x, 512 devices: a whole 4x4x16 slice. The times are simulated.
512 devices in a mesh: group: 16 (over z), dev: 32 (over y, x, core).
Axes of the slice: x: 4, y: 4, z: 16, core: 2. Of those that a mesh axis runs over, the one named last changes fastest.
Arguments:
- embeddings: float32 [1024, 128, 512], P(('group', 'dev')), may hold values from -6 to 6
- neighbours: int32 [1024, 8], P(('group', 'dev')), may hold values from 0 to 1023, as said below
Outputs:
- diffused: float32 [1024, 128, 512], P(('group', 'dev'))
Inputs may be any that keep to these rules, and one draw needn't show every extreme that they name: `neighbours`: blocks are numbered device after device in the mesh order, 2 to a device. For a block on device (g, d): entries 0 to 3 name other blocks of the same device; entries 4 to 6 name blocks of group g on devices other than d, and the blocks of one device name at most 1 block of any one other device this way, a bound that some device of every group receives from each other device of the group; the last entry names a block of group (g + 1) mod the number of groups on dev index d.
All inputs are finite; a program needn't handle non-finite values.
Results may differ from a plain program's by a relative error of at most 0.0014.
Values may be sent and summed in bfloat16 or wider, within the bound.
No kernel may reach another device: no remote copies, remote signals or barrier semaphores. Data moves between devices by JAX's collectives and lax.ppermute only.
A program may use at most 128 MiB of HBM per device.

v0:
```python
import jax
import jax.numpy as jnp
from jax import lax
from jax.sharding import PartitionSpec as P

KO = 4
KI = 3


inv_band = 40.0
eps = 1e-06


def padded(cells, sides, width):
    for axis, dim in sides:
        count = lax.axis_size(axis)
        head = lax.slice_in_dim(cells, 0, width, axis=dim)
        tail = lax.slice_in_dim(cells, cells.shape[dim] - width, cells.shape[dim], axis=dim)
        cells = jnp.concatenate(
            [
                lax.ppermute(tail, axis, [(i, (i + 1) % count) for i in range(count)]),
                cells,
                lax.ppermute(head, axis, [((i + 1) % count, i) for i in range(count)]),
            ],
            axis=dim,
        )
    return cells


def shifted(block, axis, distance):
    devices = range(lax.axis_size(axis))
    route = [((i - distance) % len(devices), i) for i in devices]
    return lax.ppermute(block, axis, route)


def row_scales(rounded):
    widened = rounded.astype(jnp.float32)
    return lax.rsqrt(jnp.mean(widened * widened, axis=-1) + eps)


def kernel_tiles(nearby, nearby_scale, remote, remote_scale):
    inner_prod = jnp.einsum("nre,nqe->nrq", nearby, remote, preferred_element_type=jnp.float32)
    return jnp.exp(
        inv_band
        * inner_prod
        * nearby_scale[:, :, None]
        * remote_scale[:, None, :]
        / nearby.shape[-1]
    )


def pulled_rows(kernel, valid_mask, remote):
    masked = kernel * valid_mask[:, None, None]
    weights = masked.astype(jnp.bfloat16)
    weighted = jnp.einsum("nrq,nqe->nre", weights, remote, preferred_element_type=jnp.float32)
    return (weighted, jnp.sum(masked, axis=2))


def spread_rows(owners, blocks, weighted, row_totals):
    onehot = (owners[:, None] == jnp.arange(blocks, dtype=jnp.int32)[None, :]).astype(jnp.float32)
    gathered_sum = jnp.einsum("nb,nre->bre", onehot, weighted, precision=lax.Precision.HIGHEST)
    gathered_deg = jnp.einsum("nb,nr->br", onehot, row_totals, precision=lax.Precision.HIGHEST)
    return (gathered_sum, gathered_deg)


def earlier_same(targets):
    entries = targets.shape[-1]
    position = jnp.arange(entries, dtype=jnp.int32)
    same_earlier = (targets[..., :, None] == targets[..., None, :]) & (
        position[None, :] < position[:, None]
    )
    return jnp.sum(same_earlier.astype(jnp.int32), axis=-1)


def local(embeddings, neighbours):
    blocks, height, features = embeddings.shape
    last_entry = KO + KI
    dev_count = lax.axis_size("dev")
    group_at = lax.axis_index("group")
    dev_at = lax.axis_index("dev")
    capacity = (blocks * KI + dev_count - 2) // (dev_count - 1)
    slot_count = dev_count * capacity
    rounded = embeddings.astype(jnp.bfloat16)
    scales = row_scales(rounded)
    first_block = (group_at * dev_count + dev_at) * blocks
    slot_ids = jnp.arange(blocks, dtype=jnp.int32)
    halo_rows = padded(rounded, (("group", 0),), blocks)
    lower_lists = shifted(neighbours, "group", 1)
    local_ids = neighbours[:, :KO] - first_block
    remote = rounded[local_ids]
    inner_prod = jnp.einsum("bre,bkqe->bkrq", rounded, remote, preferred_element_type=jnp.float32)
    kernel = jnp.exp(
        inv_band
        * inner_prod
        * scales[:, None, :, None]
        * scales[local_ids][:, :, None, :]
        / features
    )
    weights = kernel.astype(jnp.bfloat16)
    weighted_sum = jnp.einsum("bkrq,bkqe->bre", weights, remote, preferred_element_type=jnp.float32)
    backward = jnp.einsum("bkrq,bre->bkqe", weights, rounded, preferred_element_type=jnp.float32)
    degree = jnp.sum(kernel, axis=(1, 3))
    back_sum, back_deg = spread_rows(
        local_ids.reshape(-1),
        blocks,
        backward.reshape(-1, height, features),
        jnp.sum(kernel, axis=2).reshape(-1, height),
    )
    weighted_sum = weighted_sum + back_sum
    degree = degree + back_deg
    asked_ids = neighbours[:, KO : KO + KI].reshape(-1)
    asker_slot = jnp.repeat(slot_ids, KI)
    asked_dev = asked_ids // blocks % dev_count
    asked_slot = asked_ids % blocks
    placing = asked_dev * capacity + earlier_same(asked_dev)
    matches = placing[:, None] == jnp.arange(slot_count, dtype=jnp.int32)[None, :]
    filled = jnp.any(matches, axis=0)
    sent_from = jnp.sum(jnp.where(matches, asker_slot[:, None], 0), axis=0)
    outbound = rounded[sent_from]
    sent_slot = jnp.sum(jnp.where(matches, asked_slot[:, None] + 1, 0), axis=0) - 1
    wanted, pushed = (
        lax.all_to_all(
            sent_slot.reshape(dev_count, capacity), "dev", split_axis=0, concat_axis=0, tiled=True
        ),
        lax.all_to_all(
            outbound.reshape(dev_count, capacity, height, features),
            "dev",
            split_axis=0,
            concat_axis=0,
            tiled=True,
        ),
    )
    answer = rounded[jnp.maximum(wanted, 0)]
    replies = lax.all_to_all(answer, "dev", split_axis=0, concat_axis=0, tiled=True)
    replies = replies.reshape(slot_count, height, features)
    pushed = pushed.reshape(slot_count, height, features)
    wanted = wanted.reshape(-1)
    kernel = kernel_tiles(outbound, scales[sent_from], replies, row_scales(replies))
    weighted, row_totals = pulled_rows(kernel, filled.astype(jnp.float32), replies)
    add_sum, add_deg = spread_rows(sent_from, blocks, weighted, row_totals)
    weighted_sum = weighted_sum + add_sum
    degree = degree + add_deg
    targets = jnp.maximum(wanted, 0)
    kernel = kernel_tiles(rounded[targets], scales[targets], pushed, row_scales(pushed))
    weighted, row_totals = pulled_rows(kernel, (wanted >= 0).astype(jnp.float32), pushed)
    add_sum, add_deg = spread_rows(targets, blocks, weighted, row_totals)
    weighted_sum = weighted_sum + add_sum
    degree = degree + add_deg
    every_block = jnp.ones((blocks,), jnp.float32)
    upper_block = halo_rows[2 * blocks :]
    lower_block = halo_rows[:blocks]
    upper_rows = upper_block[neighbours[:, last_entry] % blocks]
    kernel = kernel_tiles(rounded, scales, upper_rows, row_scales(upper_rows))
    weighted, row_totals = pulled_rows(kernel, every_block, upper_rows)
    weighted_sum = weighted_sum + weighted
    degree = degree + row_totals
    down_slot = lower_lists[:, last_entry] % blocks
    kernel = kernel_tiles(
        rounded[down_slot], scales[down_slot], lower_block, row_scales(lower_block)
    )
    weighted, row_totals = pulled_rows(kernel, every_block, lower_block)
    add_sum, add_deg = spread_rows(down_slot, blocks, weighted, row_totals)
    weighted_sum = weighted_sum + add_sum
    degree = degree + add_deg
    return 0.5 * embeddings + 0.5 * weighted_sum / degree[:, :, None]


def solution(mesh):
    in_specs = (P(("group", "dev"), None, None), P(("group", "dev"), None))
    out_specs = P(("group", "dev"), None, None)
    return jax.shard_map(local, mesh=mesh, in_specs=in_specs, out_specs=out_specs, check_vma=False)
```

profile of v0, /device:TPU:1, one launch (start us, length us, event | category | flops | bytes accessed | tf_op | source)
XLA Modules:
  0.0 153.3 jit_solution(16718432364550447204)
XLA Ops:
  0.0 0.7 slice.13
  1.2 0.7 copy.41
  1.9 10.4 %all-to-all-start = ((s32[32,1,1]{2,1,0:T(1,128)}), s32[32,1,1]{2,1,0:T(1,128)S(1)}, u32[]{:S(2)}, u32[]{:S(2)}) async-start(s32[32,1,1]{2,1,0:T(1,128)} %copy.41), calls=%async_computation | async-start | bytes 32768 | tf_op jit(solution)/shard_map/all_to_all | solution.py:122
  12.3 1.2 multiply_reduce_fusion.4
  13.5 2.7 %gather_fusion.2 = bf16[32,128,512]{2,1,0:T(8,128)(2,1)} fusion(bf16[2,128,512]{2,1,0:T(8,128)(2,1)S(1)} %get-tuple-element.12, s32[1024]{0:T(1024)S(1)} %pad_clamp_fusion.3), kind=kCustom, calls=%fused_computation.2 | custom fusion | bytes 8388736 | tf_op jit(solution)/shard_map/gather | solution.py:119
  16.2 3.0 %all-to-all-done = s32[32,1,1]{2,1,0:T(1,128)S(1)} async-done(((s32[32,1,1]{2,1,0:T(1,128)}), s32[32,1,1]{2,1,0:T(1,128)S(1)}, u32[]{:S(2)}, u32[]{:S(2)}) %all-to-all-start) | async-done | bytes 160 | tf_op jit(solution)/shard_map/all_to_all | solution.py:122
  19.3 5.2 %all-to-all-start.2 = ((bf16[32,1,128,512]{3,2,1,0:T(8,128)(2,1)}), bf16[32,1,128,512]{3,2,1,0:T(8,128)(2,1)}, u32[]{:S(2)}, u32[]{:S(2)}) async-start(bf16[32,1,128,512]{3,2,1,0:T(8,128)(2,1)} %bitcast.90), calls=%async_computation.2 | async-start | bytes 8388608 | tf_op jit(solution)/shard_map/all_to_all | solution.py:125
  24.5 9.2 %collective-permute-start = (bf16[2,128,512]{2,1,0:T(8,128)(2,1)S(1)}, bf16[2,128,512]{2,1,0:T(8,128)(2,1)S(1)}, u32[]{:S(2)}, u32[]{:S(2)}) collective-permute-start(bf16[2,128,512]{2,1,0:T(8,128)(2,1)S(1)} %get-tuple-element.12), channel_id=1, source_target_pairs={{32,0},{64,32},{96,64},{128,96},{160,128},{192,160},{224,192},{256... | collective-permute-start | bytes 786440 | tf_op jit(solution)/shard_map/ppermute | solution.py:23
  33.8 1.9 %collective-permute-start.1 = (s32[2,8]{1,0:T(2,128)S(1)}, s32[2,8]{1,0:T(2,128)S(1)}, u32[]{:S(2)}, u32[]{:S(2)}) collective-permute-start(s32[2,8]{1,0:T(2,128)S(1)} %copy-done.3), channel_id=1, source_target_pairs={{480,0},{0,32},{32,64},{64,96},{96,128},{128,160},{160,192},{192,2... | collective-permute-start | bytes 200 | tf_op jit(solution)/shard_map/ppermute | solution.py:33
  35.7 1.9 %collective-permute-start.2 = (bf16[2,128,512]{2,1,0:T(8,128)(2,1)S(1)}, bf16[2,128,512]{2,1,0:T(8,128)(2,1)S(1)}, u32[]{:S(2)}, u32[]{:S(2)}) collective-permute-start(bf16[2,128,512]{2,1,0:T(8,128)(2,1)S(1)} %get-tuple-element.12), channel_id=1, source_target_pairs={{0,32},{32,64},{64,96},{96,128},{128,160},{160,192},{192,224},{224... | collective-permute-start | bytes 786440 | tf_op jit(solution)/shard_map/ppermute | solution.py:21
  37.6 0.6 gather_fusion.4
  38.3 0.6 gather_fusion
  39.9 0.6 fusion.71
  41.0 2.2 %fusion.12 = f32[2,128,512]{2,0,1:T(2,128)S(1)} fusion(f32[8,128,512]{2,1,0:T(8,128)S(1)} %bitcast.92, s32[8]{0:T(128)S(1)} %eq.88), kind=kOutput, calls=%fused_computation.24 | convolution fusion | flops 12582928 | bytes 2621472 | tf_op jit(solution)/shard_map/nb,nre->bre/dot_general | solution.py:61
  43.4 0.6 gather_fusion.7
  44.6 0.7 maximum_reduce_fusion
  45.3 2.8 %gather_fusion.3 = bf16[32,128,512]{2,1,0:T(8,128)(2,1)} fusion(bf16[2,128,512]{2,1,0:T(8,128)(2,1)S(1)} %get-tuple-element.12, s32[1024]{0:T(1024)S(1)} %pad_clamp_fusion.2), kind=kCustom, calls=%fused_computation.3 | custom fusion | bytes 8388736 | tf_op jit(solution)/shard_map/gather | solution.py:133
  48.0 0.6 gather_fusion.5
  48.6 26.3 %all-to-all-done.2 = bf16[32,1,128,512]{3,2,1,0:T(8,128)(2,1)} async-done(((bf16[32,1,128,512]{3,2,1,0:T(8,128)(2,1)}), bf16[32,1,128,512]{3,2,1,0:T(8,128)(2,1)}, u32[]{:S(2)}, u32[]{:S(2)}) %all-to-all-start.2) | async-done | bytes 4194336 | tf_op jit(solution)/shard_map/all_to_all | solution.py:125
  74.9 8.1 %all-to-all-start.1 = ((bf16[32,1,128,512]{3,2,1,0:T(8,128)(2,1)}), bf16[32,1,128,512]{3,2,1,0:T(8,128)(2,1)}, u32[]{:S(2)}, u32[]{:S(2)}) async-start(bf16[32,1,128,512]{3,2,1,0:T(8,128)(2,1)} %bitcast.91), calls=%async_computation.1 | async-start | bytes 8388608 | tf_op jit(solution)/shard_map/all_to_all | solution.py:134
  83.4 0.6 gather_fusion.6
  85.0 1.3 fusion.39
  86.4 3.1 %multiply_reduce_fusion = f32[32,128]{1,0:T(8,128)S(1)} fusion(bf16[32,1,128,512]{3,2,1,0:T(8,128)(2,1)} %all-to-all-done.2), kind=kLoop, calls=%fused_computation.14 | loop fusion | flops 6287360 | bytes 4210688 | tf_op jit(solution)/shard_map/reduce_sum | solution.py:38
  89.5 3.6 %fusion.75 = (f32[32,128]{1,0:T(8,128)S(1)}, bf16[32,128,128]{1,2,0:T(8,128)(2,1)S(1)}) fusion(f32[32]{0:T(128)S(1)} %fusion.49, f32[32,128]{1,0:T(8,128)S(1)} %add_rsqrt_fusion, f32[32,128]{1,0:T(8,128)S(1)} %broadcast_multiply_fusion, bf16[32,128,512]{2,1,0:T(8,128)(2,1)S(1)} %copy-done.1, bf16[32,1,128,512]{3,2,1,0:T(8,128)(2,1)} %all-to-all-done.2), kind=kOutput, calls=%fused_computation.142 | convolution fusion | flops 540012544 | bytes 9486464 | tf_op jit(solution)/shard_map/nre,nqe->nrq/dot_general | solution.py:42
  93.0 3.5 %fusion.4 = f32[32,128,512]{2,1,0:T(8,128)S(1)} fusion(bf16[32,1,128,512]{3,2,1,0:T(8,128)(2,1)} %all-to-all-done.2, bf16[32,128,128]{1,2,0:T(8,128)(2,1)S(1)} %get-tuple-element.25), kind=kOutput, calls=%fused_computation.16 | convolution fusion | flops 536870912 | bytes 13631488 | tf_op jit(solution)/shard_map/nrq,nqe->nre/dot_general | solution.py:55
  96.5 7.7 %fusion = f32[2,128,512]{2,0,1:T(2,128)S(1)} fusion(f32[32,128,512]{2,1,0:T(8,128)S(1)} %fusion.4, s32[32]{0:T(128)S(1)} %maximum_reduce_fusion), kind=kOutput, calls=%fused_computation.10 | convolution fusion | flops 50331712 | bytes 8913024 | tf_op jit(solution)/shard_map/nb,nre->bre/dot_general | solution.py:61
  104.3 29.0 %all-to-all-done.1 = bf16[32,1,128,512]{3,2,1,0:T(8,128)(2,1)} async-done(((bf16[32,1,128,512]{3,2,1,0:T(8,128)(2,1)}), bf16[32,1,128,512]{3,2,1,0:T(8,128)(2,1)}, u32[]{:S(2)}, u32[]{:S(2)}) %all-to-all-start.1) | async-done | bytes 4194336 | tf_op jit(solution)/shard_map/all_to_all | solution.py:134
  133.2 3.2 %multiply_reduce_fusion.1 = f32[32,128]{1,0:T(8,128)S(1)} fusion(bf16[32,1,128,512]{3,2,1,0:T(8,128)(2,1)} %all-to-all-done.1), kind=kLoop, calls=%fused_computation.15 | loop fusion | flops 6287360 | bytes 4210688 | tf_op jit(solution)/shard_map/reduce_sum | solution.py:38
  136.7 3.5 %fusion.74 = (f32[32,128]{1,0:T(8,128)S(1)}, bf16[32,128,128]{1,2,0:T(8,128)(2,1)S(1)}) fusion(f32[32]{0:T(128)S(1)} %convert_element_type.54, f32[32,128]{1,0:T(8,128)S(1)} %add_rsqrt_fusion.1, f32[32,128]{1,0:T(8,128)S(1)} %broadcast_multiply_fusion.1, bf16[32,128,512]{2,1,0:T(8,128)(2,1)S(1)} %copy-done, bf16[32,1,128,512]{3,2,1,0:T(8,128)(2,1)} %all-to-all-done.1), kind=kOutput, calls=%fused_computation.141 | convolution fusion | flops 540012544 | bytes 9486464 | tf_op jit(solution)/shard_map/nre,nqe->nrq/dot_general | solution.py:42
  140.2 3.5 %fusion.8 = f32[32,128,512]{2,1,0:T(8,128)S(1)} fusion(bf16[32,1,128,512]{3,2,1,0:T(8,128)(2,1)} %all-to-all-done.1, bf16[32,128,128]{1,2,0:T(8,128)(2,1)S(1)} %get-tuple-element.23), kind=kOutput, calls=%fused_computation.20 | convolution fusion | flops 536870912 | bytes 13631488 | tf_op jit(solution)/shard_map/nrq,nqe->nre/dot_general | solution.py:55
  143.7 7.5 %fusion.2 = f32[2,128,512]{2,0,1:T(2,128)S(1)} fusion(f32[32,128,512]{2,1,0:T(8,128)S(1)} %fusion.8, s32[32]{0:T(128)S(1)} %get-tuple-element.10), kind=kOutput, calls=%fused_computation.12 | convolution fusion | flops 50331712 | bytes 8913024 | tf_op jit(solution)/shard_map/nb,nre->bre/dot_general | solution.py:61
  152.2 1.1 fusion.25
  (54 shorter events, 5.4 us)
Async XLA Ops:
  1.9 17.3 %all-to-all-start = ((s32[32,1,1]{2,1,0:T(1,128)}), s32[32,1,1]{2,1,0:T(1,128)S(1)}, u32[]{:S(2)}, u32[]{:S(2)}) async-start(s32[32,1,1]{2,1,0:T(1,128)} %copy.41), calls=%async_computation | async-start | bytes 32768 | tf_op jit(solution)/shard_map/all_to_all | solution.py:122
  19.3 14.5 %copy-start.3 = (s32[2,8]{1,0:T(2,128)S(1)}, s32[2,8]{1,0:T(2,128)}, u32[]{:S(2)}) copy-start(s32[2,8]{1,0:T(2,128)} %param.3) | copy-start | bytes 196
  19.3 55.6 %all-to-all-start.2 = ((bf16[32,1,128,512]{3,2,1,0:T(8,128)(2,1)}), bf16[32,1,128,512]{3,2,1,0:T(8,128)(2,1)}, u32[]{:S(2)}, u32[]{:S(2)}) async-start(bf16[32,1,128,512]{3,2,1,0:T(8,128)(2,1)} %bitcast.90), calls=%async_computation.2 | async-start | bytes 8388608 | tf_op jit(solution)/shard_map/all_to_all | solution.py:125
  24.5 58.9 %collective-permute-start = (bf16[2,128,512]{2,1,0:T(8,128)(2,1)S(1)}, bf16[2,128,512]{2,1,0:T(8,128)(2,1)S(1)}, u32[]{:S(2)}, u32[]{:S(2)}) collective-permute-start(bf16[2,128,512]{2,1,0:T(8,128)(2,1)S(1)} %get-tuple-element.12), channel_id=1, source_target_pairs={{32,0},{64,32},{96,64},{128,96},{160,128},{192,160},{224,192},{256... | collective-permute-start | bytes 786440 | tf_op jit(solution)/shard_map/ppermute | solution.py:23
  33.8 9.5 %collective-permute-start.1 = (s32[2,8]{1,0:T(2,128)S(1)}, s32[2,8]{1,0:T(2,128)S(1)}, u32[]{:S(2)}, u32[]{:S(2)}) collective-permute-start(s32[2,8]{1,0:T(2,128)S(1)} %copy-done.3), channel_id=1, source_target_pairs={{480,0},{0,32},{32,64},{64,96},{96,128},{128,160},{160,192},{192,2... | collective-permute-start | bytes 200 | tf_op jit(solution)/shard_map/ppermute | solution.py:33
  35.7 48.4 %collective-permute-start.2 = (bf16[2,128,512]{2,1,0:T(8,128)(2,1)S(1)}, bf16[2,128,512]{2,1,0:T(8,128)(2,1)S(1)}, u32[]{:S(2)}, u32[]{:S(2)}) collective-permute-start(bf16[2,128,512]{2,1,0:T(8,128)(2,1)S(1)} %get-tuple-element.12), channel_id=1, source_target_pairs={{0,32},{32,64},{64,96},{96,128},{128,160},{160,192},{192,224},{224... | collective-permute-start | bytes 786440 | tf_op jit(solution)/shard_map/ppermute | solution.py:21
  74.9 58.3 %all-to-all-start.1 = ((bf16[32,1,128,512]{3,2,1,0:T(8,128)(2,1)}), bf16[32,1,128,512]{3,2,1,0:T(8,128)(2,1)}, u32[]{:S(2)}, u32[]{:S(2)}) async-start(bf16[32,1,128,512]{3,2,1,0:T(8,128)(2,1)} %bitcast.91), calls=%async_computation.1 | async-start | bytes 8388608 | tf_op jit(solution)/shard_map/all_to_all | solution.py:134
  83.9 5.5 %copy-start.1 = (bf16[32,128,512]{2,1,0:T(8,128)(2,1)S(1)}, bf16[32,128,512]{2,1,0:T(8,128)(2,1)}, u32[]{:S(2)}) copy-start(bf16[32,128,512]{2,1,0:T(8,128)(2,1)} %gather_fusion.3) | copy-start | bytes 12582916
  133.2 3.4 %copy-start = (bf16[32,128,512]{2,1,0:T(8,128)(2,1)S(1)}, bf16[32,128,512]{2,1,0:T(8,128)(2,1)}, u32[]{:S(2)}) copy-start(bf16[32,128,512]{2,1,0:T(8,128)(2,1)} %gather_fusion.2) | copy-start | bytes 12582916
  143.7 8.5 %copy-start.2 = (f32[2,128,512]{2,1,0:T(8,128)S(1)}, f32[2,128,512]{2,1,0:T(8,128)}, u32[]{:S(2)}) copy-start(f32[2,128,512]{2,1,0:T(8,128)} %param.2) | copy-start | bytes 1572868
where the time goes:
time: 154 us; the launch traced here: 153 us
  waiting for transfers between devices  58.3 us (38%)
  starting transfers between devices  36.8 us (24%)
  matrix products  36.8 us (24%)
  local copies, waits for them, and re-layouts  11.5 us (7%)
  other arithmetic  9.6 us (6%)
    all_to_all x1, waiting for transfers between devices, local(): lax.all_to_all(answer, 'dev', split_axis=0, concat_axis=0, tiled=True)  29 us
    all_to_all x1, waiting for transfers between devices, local(): lax.all_to_all(outbound.reshape(dev_count, capacity, height, features), '...  26.3 us
    dot_general x4, matrix products, spread_rows(): jnp.einsum('nb,nre->bre', onehot, weighted, precision=lax.Precision.HIGHEST)  18.8 us
    all_to_all x1, starting transfers between devices, local(): lax.all_to_all(sent_slot.reshape(dev_count, capacity), 'dev', split_axis=...  10.4 us
    ppermute x1, starting transfers between devices, padded(): lax.ppermute(head, axis, [((i + 1) % count, i) for i in range(count)])  9.24 us
    dot_general x4, matrix products, pulled_rows(): jnp.einsum('nrq,nqe->nre', weights, remote, preferred_element_type=jnp.fl...  8.32 us
    all_to_all x1, starting transfers between devices, local(): lax.all_to_all(answer, 'dev', split_axis=0, concat_axis=0, tiled=True)  8.13 us
    reduce_sum x5, other arithmetic, row_scales(): return lax.rsqrt(jnp.mean(widened * widened, axis=-1) + eps)  7.75 us
  transfers between devices with their start and end apart: 6, of which 3 were waited for; matrix products, arithmetic and copies ran while one was open for 23% of the time, Pallas kernels for 0%

commit v1 on v0

v1 whole, which is shorter than its diff:
```python
import jax
import jax.numpy as jnp
from jax import lax
from jax.experimental import pallas as pl
from jax.experimental.pallas import tpu as pltpu
from jax.sharding import PartitionSpec as P

KO = 4
KI = 3
R = 128
E = 512
SIDE = 4
ROWS = 2 * R + 8
ORDER = (3, 1, 2)
TOGETHER = 4

inv_band = 40.0
eps = 1e-06

f32 = jnp.float32
bf16 = jnp.bfloat16


def whole():
    return pl.BlockSpec(memory_space=pltpu.VMEM)


def scalars():
    return pl.BlockSpec(memory_space=pltpu.SMEM)


def call(kernel, out_shape, in_specs, flops, nbytes, scratch=()):
    return pl.pallas_call(
        kernel,
        out_shape=out_shape,
        in_specs=in_specs,
        scratch_shapes=scratch,
        out_specs=jax.tree.map(lambda _: whole(), out_shape),
        cost_estimate=pl.CostEstimate(flops=flops, bytes_accessed=nbytes, transcendentals=0),
        compiler_params=pltpu.CompilerParams(vmem_limit_bytes=16 << 20),
    )


def array(shape, dtype):
    return jax.ShapeDtypeStruct(shape, dtype)


def pack_kernel(lists, rows, packed, names_at, rows_at, sems):
    copies = [
        pltpu.make_async_copy(rows.at[n // 2, at], rows_at.at[n // 2, at], sems.at[n])
        for n in range(4)
        for at in (pl.ds(n % 2 * (R // 2), R // 2),)
    ]
    listing = pltpu.make_async_copy(lists, names_at, sems.at[4])
    listing.start()
    for copy in copies:
        copy.start()
    listing.wait()
    at = lax.broadcasted_iota(jnp.int32, (8, E), 0)
    names = jnp.zeros((8, E), jnp.int32)
    for b in range(2):
        for j in range(KI + 1):
            name = names_at[b, KO + j]
            name = name % 64 if j < KI else name % 2
            names = jnp.where(at == 4 * b + j, name, names)
    packed[2 * R :, :] = names.astype(f32).astype(bf16)
    for n, copy in enumerate(copies):
        copy.wait()
        half = n % 2 * (R // 2)
        packed[n * (R // 2) : (n + 1) * (R // 2), :] = rows_at[n // 2, half : half + R // 2].astype(bf16)


def column_scale(q):
    wide = q.astype(f32)
    return lax.rsqrt(jnp.sum(wide * wide, axis=1, keepdims=True) * (1.0 / E) + eps)


def tiles(jobs, turned, scale, sums):
    weighted = []
    for q, p, times in jobs:
        inner = jnp.dot(q, turned[p], preferred_element_type=f32)
        kernel = jnp.exp(inner * column_scale(q) * scale[p, 0:1, :])
        weighted.append(kernel * times)
    pulled = [
        lax.dot_general(
            w.astype(bf16), q, (((0,), (0,)), ((), ())), preferred_element_type=f32
        )
        for (q, p, times), w in zip(jobs, weighted)
    ]
    for (q, p, times), w, rows in zip(jobs, weighted, pulled):
        sums[p, R : R + 1, :R] += jnp.sum(w, axis=0, keepdims=True)
        sums[p, :R, :] += rows


def local_kernel(own, other, turned, scale, asked, sums):
    lane = lax.broadcasted_iota(jnp.int32, (1, E), 1) // R
    for n, (rows, b) in enumerate(((own, 0), (own, 1), (other, 0), (other, 1))):
        block = rows[b * R : (b + 1) * R, :]
        turned[n] = block.T
        column = column_scale(block) * (inv_band / E)
        scale[n] = jnp.broadcast_to(column, (R, R)).T[:8]
    own_names = own[2 * R :, :].astype(f32)
    other_names = other[2 * R :, :].astype(f32)
    for j in range(KI):
        asked[j : j + 1, :] = jnp.where(
            lane < 2,
            jnp.where(lane == 0, own_names[j : j + 1], own_names[4 + j : 5 + j]),
            jnp.where(lane == 2, other_names[j : j + 1], other_names[4 + j : 5 + j]),
        )
    sums[...] = jnp.zeros(sums.shape, f32)
    tiles(
        [(own[(1 - b) * R : (2 - b) * R, :], b, 2.0 * KO) for b in range(2)],
        turned,
        scale,
        sums,
    )


def across_kernel(place, own, other, across, turned, scale, sums_in, sums):
    sums[...] = sums_in[...]
    upper = place[1] == 1
    jobs = []
    for n, rows in enumerate((own, other)):
        near_names = rows[2 * R :, :].astype(f32)
        far_names = across[n, 2 * R :, :].astype(f32)
        for b in range(2):
            row = 4 * b + KI
            ours = jnp.max(near_names[row : row + 1, :R]).astype(jnp.int32)
            named = jnp.max(far_names[row : row + 1, :R]).astype(jnp.int32)
            far = jnp.clip(jnp.where(upper, ours, b), 0, 1)
            near = jnp.clip(jnp.where(upper, b, named), 0, 1)
            q = across[n, pl.ds(pl.multiple_of(far * R, R), R), :]
            jobs.append((q, 2 * n + near, 1.0))
    tiles(jobs, turned, scale, sums)


def partner(at, swap):
    near = at + 1 - 2 * (at % 2)
    away = SIDE - 1 - at
    return jnp.where(swap == 0, at, jnp.where(swap == 1, near, jnp.where(swap == 2, away, (at + 2) % SIDE)))


def pairs_of(far, second, place, asked, jobs):
    dev = place[0]
    y, x, core = dev // 8, dev // 2 % SIDE, dev % 2
    lane = lax.broadcasted_iota(jnp.int32, (1, E), 1) // R
    code = jnp.where(lane < 2, dev * 2 + lane, (dev + 1 - 2 * core) * 2 + lane - 2).astype(f32)
    digits = jnp.zeros((1, E), f32)
    for k, first in enumerate((0,) + ORDER):
        from_x = partner(x, jnp.where(core == 0, first, second))
        from_y = partner(y, jnp.where(core == 0, second, first))
        source = (from_y * SIDE + from_x) * 2 + core
        names = far[k, 2 * R :, :].astype(f32)
        for b in range(2):
            block = (source * 2 + b).astype(f32)
            count = jnp.zeros((1, E), f32)
            for j in range(KI):
                count += jnp.where(names[4 * b + j : 4 * b + j + 1] == code, 1.0, 0.0)
                count += jnp.where(asked[j : j + 1, :] == block, 1.0, 0.0)
            digits += count * float(4 ** (2 * k + b))
    total = jnp.int32(0)
    for p in range(4):
        word = jnp.max(digits[:, p * R : (p + 1) * R]).astype(jnp.int32)
        for n in range(2 * SIDE):
            times = (word >> (2 * n)) & 3
            jobs[0, total] = n
            jobs[1, total] = p
            jobs[2, total] = times
            total = total + jnp.where(times > 0, 1, 0)
    for n in range(TOGETHER - 1):
        jobs[0, total + n] = 0
        jobs[1, total + n] = 0
        jobs[2, total + n] = 0
    return total


def add_far(far, second, place, turned, scale, asked, sums, jobs):
    total = pairs_of(far, second, place, asked, jobs)

    def some(i, carry):
        taken = []
        for t in range(TOGETHER):
            n, p, times = (jobs[row, i * TOGETHER + t] for row in range(3))
            q = far[n // 2, pl.ds(pl.multiple_of(n % 2 * R, R), R), :]
            taken.append((q, p, times.astype(f32)))
        tiles(taken, turned, scale, sums)
        return carry

    lax.fori_loop(0, (total + TOGETHER - 1) // TOGETHER, some, 0)


def far_kernel(seconds, place, *refs):
    far = refs[: len(seconds)]
    turned, scale, asked, sums_in, sums = refs[len(seconds) : len(seconds) + 5]
    jobs = refs[-1]
    sums[...] = sums_in[...]
    for rows, second in zip(far, seconds):
        add_far(rows, second, place, turned, scale, asked, sums, jobs)
    for theirs in refs[len(seconds) + 5 : -1]:
        theirs[...] = sums[2:]


def finish_kernel(rows, sums, received, out):
    for b in range(2):
        degree = sums[b, R : R + 1, :R] + received[b, R : R + 1, :R]
        column = jnp.broadcast_to(0.5 / degree, (R, R)).T
        for t in range(E // R):
            at = slice(t * R, (t + 1) * R)
            pulled = sums[b, :R, at] + received[b, :R, at]
            out[b, :, at] = 0.5 * rows[b, :, at] + pulled * column


def swaps(stage, swap):
    to = {1: (1, 0, 3, 2), 2: (3, 2, 1, 0), 3: (2, 3, 0, 1)}[swap]
    pairs = []
    for y in range(SIDE):
        for x in range(SIDE):
            for core in range(2):
                along_x = (core + stage) % 2 == 0
                to_x, to_y = (to[x], y) if along_x else (x, to[y])
                pairs.append(((y * SIDE + x) * 2 + core, (to_y * SIDE + to_x) * 2 + core))
    return pairs


def across_swaps(groups, devices):
    pairs = []
    for z in range(groups):
        for dev in range(devices):
            to = (z + 1 if (z + dev) % 2 == 0 else z - 1) % groups
            pairs.append((z * devices + dev, to * devices + dev))
    return pairs


def local(embeddings, neighbours):
    groups, devices = lax.axis_size("group"), lax.axis_size("dev")
    dev = lax.axis_index("dev").astype(jnp.int32)
    upper = (lax.axis_index("group").astype(jnp.int32) + dev) % 2 == 0
    place = jnp.where(jnp.arange(2) == 0, dev, upper.astype(jnp.int32))
    packed = pl.pallas_call(
        pack_kernel,
        out_shape=array((ROWS, E), bf16),
        in_specs=[pl.BlockSpec(memory_space=pltpu.HBM)] * 2,
        out_specs=whole(),
        scratch_shapes=[
            pltpu.SMEM(neighbours.shape, jnp.int32),
            pltpu.VMEM(embeddings.shape, f32),
            pltpu.SemaphoreType.DMA((5,)),
        ],
        cost_estimate=pl.CostEstimate(flops=1 << 18, bytes_accessed=3 << 18, transcendentals=0),
        compiler_params=pltpu.CompilerParams(vmem_limit_bytes=60 << 20),
    )(neighbours, embeddings)

    def along(value, stage, swap):
        return lax.ppermute(value, "dev", swaps(stage, swap))

    between = [(i, i ^ 1) for i in range(devices)]
    near = [along(packed, 0, swap) for swap in ORDER]
    other = lax.ppermute(packed, "dev", between)
    across = lax.ppermute(
        jnp.stack([packed, other]), ("group", "dev"), across_swaps(groups, devices)
    )
    near = jnp.stack([packed] + near)
    far = [along(near, 1, swap) for swap in ORDER]

    all_sums = array((4, R + 8, E), f32)
    turned, scale, asked, sums = call(
        local_kernel,
        (array((4, E, R), bf16), array((4, 8, R), f32), array((8, E), f32), all_sums),
        [whole()] * 2,
        200_000_000,
        2 << 20,
    )(packed, other)

    def add(rows, seconds, sums, last):
        def kernel(*refs):
            far_kernel(seconds, *refs)

        return call(
            kernel,
            (all_sums,) + (array((2, R + 8, E), f32),) * last,
            [scalars()] + [whole()] * (len(rows) + 4),
            200_000_000,
            2 << 20,
            [pltpu.SMEM((3, 8 * SIDE + TOGETHER), jnp.int32)],
        )(place, *rows, turned, scale, asked, sums)

    (sums,) = add([near], (0,), sums, 0)
    (sums,) = add(far[:1], ORDER[:1], sums, 0)
    sums = call(
        across_kernel, all_sums, [scalars()] + [whole()] * 6, 200_000_000, 2 << 20
    )(place, packed, other, across, turned, scale, sums)
    sums, theirs = add(far[1:], ORDER[1:], sums, 1)
    received = lax.ppermute(theirs, "dev", between)
    return call(
        finish_kernel,
        array(embeddings.shape, f32),
        [whole()] * 3,
        1 << 20,
        2 << 20,
    )(embeddings, sums, received)


def solution(mesh):
    in_specs = (P(("group", "dev"), None, None), P(("group", "dev"), None))
    out_specs = P(("group", "dev"), None, None)
    return jax.shard_map(local, mesh=mesh, in_specs=in_specs, out_specs=out_specs, check_vma=False)
```

time: 154 us -> 63.9 us (0.41)
  waiting for transfers between devices: 58.3 us -> 12.4 us
  matrix products: 36.8 us -> 0 us
  Pallas kernels: 0 us -> 11.5 us
  local copies, waits for them, and re-layouts: 11.5 us -> 0.01 us
  other arithmetic: 9.6 us -> 2.03 us
    all_to_all x3 -> x0, waiting for transfers between devices: 58.3 us -> none  [the longest x1 29 us: local(): lax.all_to_all(answer, 'dev', split_axis=0, concat_axis=0, tiled=True)]
    dot_general x19 -> x0, matrix products: 36.8 us -> none  [the longest x4 18.8 us: spread_rows(): jnp.einsum('nb,nre->bre', onehot, weighted, precision=lax.Precision.HIGHEST)]
    ppermute x3 -> x9, starting transfers between devices: 13.1 us -> 37.3 us  [the longest x6 19.6 us: along(): return lax.ppermute(value, 'dev', swaps(stage, swap))]
    all_to_all x3 -> x0, starting transfers between devices: 23.7 us -> none  [the longest x1 10.4 us: local(): lax.all_to_all(sent_slot.reshape(dev_count, capacity), 'dev', split_axis=...]
    ppermute x3 -> x9, waiting for transfers between devices: 0.01 us -> 12.4 us  [the longest x6 6.32 us: along(): return lax.ppermute(value, 'dev', swaps(stage, swap))]
    pallas_call x0 -> x7, Pallas kernels: none -> 11.5 us  [the longest x3 6.8 us: add(): call(kernel, (all_sums,) + (array((2, R + 8, E), f32),) * last, [scalars(...]
    gather x9 -> x0, local copies, waits for them, and re-layouts: 9.52 us -> none  [the longest x1 2.78 us: local(): answer = rounded[jnp.maximum(wanted, 0)]]
    reduce_sum x7 -> x0, other arithmetic: 8.02 us -> none  [the longest x5 7.75 us: row_scales(): return lax.rsqrt(jnp.mean(widened * widened, axis=-1) + eps)]
  transfers between devices with their start and end apart: 6 -> 9, of which waited for: 3 -> 5; matrix products, arithmetic and copies ran while one was open for 23% -> 1% of each run, Pallas kernels for 0% -> 9%
where the time goes in v1:
time: 63.9 us; the launch traced here: 63.5 us
  starting transfers between devices  37.3 us (58%)
  waiting for transfers between devices  12.4 us (19%)
  Pallas kernels  11.5 us (18%)
  other arithmetic  2.03 us (3%)
    ppermute x6, starting transfers between devices, along(): return lax.ppermute(value, 'dev', swaps(stage, swap))  19.6 us
    ppermute x1, starting transfers between devices, local(): lax.ppermute(jnp.stack([packed, other]), ('group', 'dev'), across_swaps(g...  8.65 us
    ppermute x1, starting transfers between devices, local(): other = lax.ppermute(packed, 'dev', between)  7.14 us
    pallas_call x3, Pallas kernels, add(): call(kernel, (all_sums,) + (array((2, R + 8, E), f32),) * last, [scalars(...  6.8 us
    ppermute x6, waiting for transfers between devices, along(): return lax.ppermute(value, 'dev', swaps(stage, swap))  6.32 us
    ppermute x1, waiting for transfers between devices, local(): lax.ppermute(jnp.stack([packed, other]), ('group', 'dev'), across_swaps(g...  3 us
    ppermute x1, waiting for transfers between devices, local(): received = lax.ppermute(theirs, 'dev', between)  1.92 us
    ppermute x1, starting transfers between devices, local(): received = lax.ppermute(theirs, 'dev', between)  1.92 us
  transfers between devices with their start and end apart: 9, of which 5 were waited for; matrix products, arithmetic and copies ran while one was open for 1% of the time, Pallas kernels for 9%

profile of v1, /device:TPU:1, one launch (start us, length us, event | category | flops | bytes accessed | tf_op | source)
XLA Modules:
  0.0 63.5 jit_solution(10643739226353036219)
XLA Ops:
  0.0 1.8 %shard_map.28.own = bf16[264,512]{1,0:T(8,128)(2,1)} custom-call(s32[2,8]{1,0:T(2,128)} %lists.1, f32[2,128,512]{2,1,0:T(8,128)} %rows.3), custom_call_target="tpu_custom_call" | custom-call | flops 262144 | bytes 786432 | tf_op jit(solution)/shard_map/pallas_call | solution.py:239
  1.9 5.7 %collective-permute-start = (bf16[264,512]{1,0:T(8,128)(2,1)}, bf16[264,512]{1,0:T(8,128)(2,1)S(1)}, u32[]{:S(2)}, u32[]{:S(2)}) collective-permute-start(bf16[264,512]{1,0:T(8,128)(2,1)} %shard_map.28.own), channel_id=1, source_target_pairs={{0,4},{1,17},{2,6},{3,19},{4,0},{5,21},{6,2},{7,23},{8,12},{9,25},... | collective-permute-start | bytes 811016 | tf_op jit(solution)/shard_map/ppermute | solution.py:254
  7.5 2.3 %collective-permute-start.1 = (bf16[264,512]{1,0:T(8,128)(2,1)}, bf16[264,512]{1,0:T(8,128)(2,1)S(1)}, u32[]{:S(2)}, u32[]{:S(2)}) collective-permute-start(bf16[264,512]{1,0:T(8,128)(2,1)} %shard_map.28.own), channel_id=1, source_target_pairs={{0,2},{1,9},{2,0},{3,11},{4,6},{5,13},{6,4},{7,15},{8,10},{9,1},{1... | collective-permute-start | bytes 811016 | tf_op jit(solution)/shard_map/ppermute | solution.py:254
  9.8 2.3 %collective-permute-start.2 = (bf16[264,512]{1,0:T(8,128)(2,1)}, bf16[264,512]{1,0:T(8,128)(2,1)S(1)}, u32[]{:S(2)}, u32[]{:S(2)}) collective-permute-start(bf16[264,512]{1,0:T(8,128)(2,1)} %shard_map.28.own), channel_id=1, source_target_pairs={{0,6},{1,25},{2,4},{3,27},{4,2},{5,29},{6,0},{7,31},{8,14},{9,17},... | collective-permute-start | bytes 811016 | tf_op jit(solution)/shard_map/ppermute | solution.py:254
  12.1 0.0 collective-permute-done
  12.1 2.8 %collective-permute-done.1 = bf16[264,512]{1,0:T(8,128)(2,1)S(1)} collective-permute-done((bf16[264,512]{1,0:T(8,128)(2,1)}, bf16[264,512]{1,0:T(8,128)(2,1)S(1)}, u32[]{:S(2)}, u32[]{:S(2)}) %collective-permute-start.1) | collective-permute-done | bytes 270368 | tf_op jit(solution)/shard_map/ppermute | solution.py:254
  14.9 3.5 %collective-permute-done.2 = bf16[264,512]{1,0:T(8,128)(2,1)S(1)} collective-permute-done((bf16[264,512]{1,0:T(8,128)(2,1)}, bf16[264,512]{1,0:T(8,128)(2,1)S(1)}, u32[]{:S(2)}, u32[]{:S(2)}) %collective-permute-start.2) | collective-permute-done | bytes 270368 | tf_op jit(solution)/shard_map/ppermute | solution.py:254
  18.5 0.0 copy-start
  18.5 1.2 %pad_maximum_fusion.refs_1_ = bf16[4,264,512]{2,1,0:T(8,128)(2,1)S(1)} fusion(bf16[1,264,512]{2,1,0:T(8,128)(2,1)S(1)} %bitcast.10, bf16[1,264,512]{2,1,0:T(8,128)(2,1)S(1)} %bitcast.9, bf16[1,264,512]{2,1,0:T(8,128)(2,1)S(1)} %bitcast.8, bf16[1,264,512]{2,1,0:T(8,128)(2,1)} %bitcast.5), kind=kLoop, calls=%fused_computation | loop fusion | flops 1622016 | bytes 2162688 | tf_op jit(solution)/shard_map/stack | solution.py:262
  19.6 4.7 %collective-permute-start.7 = (bf16[4,264,512]{2,1,0:T(8,128)(2,1)S(1)}, bf16[4,264,512]{2,1,0:T(8,128)(2,1)}, u32[]{:S(2)}, u32[]{:S(2)}) collective-permute-start(bf16[4,264,512]{2,1,0:T(8,128)(2,1)S(1)} %pad_maximum_fusion.refs_1_), channel_id=1, source_target_pairs={{0,16},{1,5},{2,18},{3,7},{4,20},{5,1},{6,22},{7,3},{8,24},{9,13},... | collective-permute-start | bytes 3244040 | tf_op jit(solution)/shard_map/ppermute | solution.py:254
  24.3 2.2 %collective-permute-start.3 = (bf16[4,264,512]{2,1,0:T(8,128)(2,1)S(1)}, bf16[4,264,512]{2,1,0:T(8,128)(2,1)S(1)}, u32[]{:S(2)}, u32[]{:S(2)}) collective-permute-start(bf16[4,264,512]{2,1,0:T(8,128)(2,1)S(1)} %pad_maximum_fusion.refs_1_), channel_id=1, source_target_pairs={{0,8},{1,3},{2,10},{3,1},{4,12},{5,7},{6,14},{7,5},{8,0},{9,11},{1... | collective-permute-start | bytes 3244040 | tf_op jit(solution)/shard_map/ppermute | solution.py:254
  26.5 2.5 %collective-permute-start.4 = (bf16[4,264,512]{2,1,0:T(8,128)(2,1)S(1)}, bf16[4,264,512]{2,1,0:T(8,128)(2,1)}, u32[]{:S(2)}, u32[]{:S(2)}) collective-permute-start(bf16[4,264,512]{2,1,0:T(8,128)(2,1)S(1)} %pad_maximum_fusion.refs_1_), channel_id=1, source_target_pairs={{0,24},{1,7},{2,26},{3,5},{4,28},{5,3},{6,30},{7,1},{8,16},{9,15},... | collective-permute-start | bytes 3244040 | tf_op jit(solution)/shard_map/ppermute | solution.py:254
  29.0 0.0 copy-done
  29.0 7.1 %collective-permute-start.5 = (bf16[264,512]{1,0:T(8,128)(2,1)S(1)}, bf16[264,512]{1,0:T(8,128)(2,1)S(1)}, u32[]{:S(2)}, u32[]{:S(2)}) collective-permute-start(bf16[264,512]{1,0:T(8,128)(2,1)S(1)} %copy-done), channel_id=1, source_target_pairs={{0,1},{1,0},{2,3},{3,2},{4,5},{5,4},{6,7},{7,6},{8,9},{9,8},{10,11... | collective-permute-start | bytes 811016 | tf_op jit(solution)/shard_map/ppermute | solution.py:258
  36.1 1.2 %collective-permute-done.5.other = bf16[264,512]{1,0:T(8,128)(2,1)S(1)} collective-permute-done((bf16[264,512]{1,0:T(8,128)(2,1)S(1)}, bf16[264,512]{1,0:T(8,128)(2,1)S(1)}, u32[]{:S(2)}, u32[]{:S(2)}) %collective-permute-start.5) | collective-permute-done | bytes 270368 | tf_op jit(solution)/shard_map/ppermute | solution.py:258
  37.3 0.9 %pad_maximum_fusion.1 = bf16[2,264,512]{2,1,0:T(8,128)(2,1)} fusion(bf16[1,264,512]{2,1,0:T(8,128)(2,1)S(1)} %bitcast.7, bf16[1,264,512]{2,1,0:T(8,128)(2,1)S(1)} %bitcast.6), kind=kLoop, calls=%fused_computation.1 | loop fusion | flops 270336 | bytes 1081344 | tf_op jit(solution)/shard_map/stack | solution.py:260
  38.2 8.7 %collective-permute-start.6 = (bf16[2,264,512]{2,1,0:T(8,128)(2,1)}, bf16[2,264,512]{2,1,0:T(8,128)(2,1)S(1)}, u32[]{:S(2)}, u32[]{:S(2)}) collective-permute-start(bf16[2,264,512]{2,1,0:T(8,128)(2,1)} %pad_maximum_fusion.1), channel_id=1, source_target_pairs={{0,32},{1,481},{2,34},{3,483},{4,36},{5,485},{6,38},{7,487},{8,40}... | collective-permute-start | bytes 1622024 | tf_op jit(solution)/shard_map/ppermute | solution.py:259
  46.8 0.7 %shard_map.29 = (bf16[4,512,128]{2,1,0:T(8,128)(2,1)S(1)}, f32[4,8,128]{2,1,0:T(8,128)S(1)}, f32[8,512]{1,0:T(8,128)S(1)}, f32[4,136,512]{2,1,0:T(8,128)S(1)}) custom-call(bf16[264,512]{1,0:T(8,128)(2,1)S(1)} %copy-done, bf16[264,512]{1,0:T(8,128)(2,1)S(1)} %collective-permute-done.5.other), custom_call_target="tpu_custom_call" | custom-call | flops 200000000 | bytes 2097152 | tf_op jit(solution)/shard_map/pallas_call | solution.py:266
  47.5 1.5 %shard_map.30.refs_5_ = f32[4,136,512]{2,1,0:T(8,128)S(1)} custom-call(s32[2]{0:T(128)S(1)} %compare_select_fusion.refs_0_.place, bf16[4,264,512]{2,1,0:T(8,128)(2,1)S(1)} %pad_maximum_fusion.refs_1_, bf16[4,512,128]{2,1,0:T(8,128)(2,1)S(1)} %get-tuple-element.11.refs_2_.turned.refs_3_, f32[4,8,128]{2,1,0:T(8,128)S(1)} %get-tuple-element.12.refs_3_.scale.refs_4_, ...), custom_call_target="tpu_custom_call" | custom-call | flops 200000000 | bytes 2097152 | tf_op jit(solution)/shard_map/pallas_call | solution.py:278
  49.0 0.0 collective-permute-done.7.refs_1_
  49.0 2.2 %shard_map.31.sums_in = f32[4,136,512]{2,1,0:T(8,128)S(1)} custom-call(s32[2]{0:T(128)S(1)} %compare_select_fusion.refs_0_.place, bf16[4,264,512]{2,1,0:T(8,128)(2,1)} %collective-permute-done.7.refs_1_, bf16[4,512,128]{2,1,0:T(8,128)(2,1)S(1)} %get-tuple-element.11.refs_2_.turned.refs_3_, f32[4,8,128]{2,1,0:T(8,128)S(1)} %get-tuple-element.12.refs_3_.scale.refs_4_, ...), custom_call_target="tpu_custom_call" | custom-call | flops 200000000 | bytes 2097152 | tf_op jit(solution)/shard_map/pallas_call | solution.py:278
  51.2 3.0 %collective-permute-done.6.across = bf16[2,264,512]{2,1,0:T(8,128)(2,1)S(1)} collective-permute-done((bf16[2,264,512]{2,1,0:T(8,128)(2,1)}, bf16[2,264,512]{2,1,0:T(8,128)(2,1)S(1)}, u32[]{:S(2)}, u32[]{:S(2)}) %collective-permute-start.6) | collective-permute-done | bytes 540704 | tf_op jit(solution)/shard_map/ppermute | solution.py:259
  54.2 1.2 %shard_map.32.refs_6_ = f32[4,136,512]{2,1,0:T(8,128)S(1)} custom-call(s32[2]{0:T(128)S(1)} %compare_select_fusion.refs_0_.place, bf16[264,512]{1,0:T(8,128)(2,1)S(1)} %copy-done, bf16[264,512]{1,0:T(8,128)(2,1)S(1)} %collective-permute-done.5.other, bf16[2,264,512]{2,1,0:T(8,128)(2,1)S(1)} %collective-permute-done.6.across, ...), custom_call_target="tpu_custom_call" | custom-call | flops 200000000 | bytes 2097152 | tf_op jit(solution)/shard_map/pallas_call | solution.py:289
  55.4 0.0 copy-start.1
  55.4 0.0 collective-permute-done.3.refs_1_
  55.4 0.0 collective-permute-done.4.refs_2_
  55.4 3.2 %shard_map.33 = (f32[4,136,512]{2,1,0:T(8,128)S(1)}, f32[2,136,512]{2,1,0:T(8,128)S(1)}) custom-call(s32[2]{0:T(128)S(1)} %compare_select_fusion.refs_0_.place, bf16[4,264,512]{2,1,0:T(8,128)(2,1)S(1)} %collective-permute-done.3.refs_1_, bf16[4,264,512]{2,1,0:T(8,128)(2,1)} %collective-permute-done.4.refs_2_, ...), custom_call_target="tpu_custom_call" | custom-call | flops 200000000 | bytes 2097152 | tf_op jit(solution)/shard_map/pallas_call | solution.py:278
  58.6 1.9 %collective-permute-start.8 = (f32[2,136,512]{2,1,0:T(8,128)S(1)}, f32[2,136,512]{2,1,0:T(8,128)S(1)}, u32[]{:S(2)}, u32[]{:S(2)}) collective-permute-start(f32[2,136,512]{2,1,0:T(8,128)S(1)} %get-tuple-element.16), channel_id=1, source_target_pairs={{0,1},{1,0},{2,3},{3,2},{4,5},{5,4},{6,7},{7,6},{8,9},{9,8},{10,11... | collective-permute-start | bytes 1671176 | tf_op jit(solution)/shard_map/ppermute | solution.py:293
  60.6 1.9 %collective-permute-done.8.received = f32[2,136,512]{2,1,0:T(8,128)S(1)} collective-permute-done((f32[2,136,512]{2,1,0:T(8,128)S(1)}, f32[2,136,512]{2,1,0:T(8,128)S(1)}, u32[]{:S(2)}, u32[]{:S(2)}) %collective-permute-start.8) | collective-permute-done | bytes 557088 | tf_op jit(solution)/shard_map/ppermute | solution.py:293
  62.5 0.0 copy-done.1
  62.5 1.0 %shard_map.34 = f32[2,128,512]{2,1,0:T(8,128)} custom-call(f32[2,128,512]{2,1,0:T(8,128)S(1)} %copy-done.1, f32[4,136,512]{2,1,0:T(8,128)S(1)} %get-tuple-element.15.sums, f32[2,136,512]{2,1,0:T(8,128)S(1)} %collective-permute-done.8.received), custom_call_target="tpu_custom_call" | custom-call | flops 1048576 | bytes 2097152 | tf_op jit(solution)/shard_map/pallas_call | solution.py:294
  (1 shorter events, 0.0 us)
Async XLA Ops:
  1.9 10.3 %collective-permute-start = (bf16[264,512]{1,0:T(8,128)(2,1)}, bf16[264,512]{1,0:T(8,128)(2,1)S(1)}, u32[]{:S(2)}, u32[]{:S(2)}) collective-permute-start(bf16[264,512]{1,0:T(8,128)(2,1)} %shard_map.28.own), channel_id=1, source_target_pairs={{0,4},{1,17},{2,6},{3,19},{4,0},{5,21},{6,2},{7,23},{8,12},{9,25},... | collective-permute-start | bytes 811016 | tf_op jit(solution)/shard_map/ppermute | solution.py:254
  7.5 7.4 %collective-permute-start.1 = (bf16[264,512]{1,0:T(8,128)(2,1)}, bf16[264,512]{1,0:T(8,128)(2,1)S(1)}, u32[]{:S(2)}, u32[]{:S(2)}) collective-permute-start(bf16[264,512]{1,0:T(8,128)(2,1)} %shard_map.28.own), channel_id=1, source_target_pairs={{0,2},{1,9},{2,0},{3,11},{4,6},{5,13},{6,4},{7,15},{8,10},{9,1},{1... | collective-permute-start | bytes 811016 | tf_op jit(solution)/shard_map/ppermute | solution.py:254
  9.8 8.6 %collective-permute-start.2 = (bf16[264,512]{1,0:T(8,128)(2,1)}, bf16[264,512]{1,0:T(8,128)(2,1)S(1)}, u32[]{:S(2)}, u32[]{:S(2)}) collective-permute-start(bf16[264,512]{1,0:T(8,128)(2,1)} %shard_map.28.own), channel_id=1, source_target_pairs={{0,6},{1,25},{2,4},{3,27},{4,2},{5,29},{6,0},{7,31},{8,14},{9,17},... | collective-permute-start | bytes 811016 | tf_op jit(solution)/shard_map/ppermute | solution.py:254
  18.5 10.5 %copy-start = (bf16[264,512]{1,0:T(8,128)(2,1)S(1)}, bf16[264,512]{1,0:T(8,128)(2,1)}, u32[]{:S(2)}) copy-start(bf16[264,512]{1,0:T(8,128)(2,1)} %shard_map.28.own) | copy-start | bytes 811012
  19.6 29.4 %collective-permute-start.7 = (bf16[4,264,512]{2,1,0:T(8,128)(2,1)S(1)}, bf16[4,264,512]{2,1,0:T(8,128)(2,1)}, u32[]{:S(2)}, u32[]{:S(2)}) collective-permute-start(bf16[4,264,512]{2,1,0:T(8,128)(2,1)S(1)} %pad_maximum_fusion.refs_1_), channel_id=1, source_target_pairs={{0,16},{1,5},{2,18},{3,7},{4,20},{5,1},{6,22},{7,3},{8,24},{9,13},... | collective-permute-start | bytes 3244040 | tf_op jit(solution)/shard_map/ppermute | solution.py:254
  24.3 31.1 %collective-permute-start.3 = (bf16[4,264,512]{2,1,0:T(8,128)(2,1)S(1)}, bf16[4,264,512]{2,1,0:T(8,128)(2,1)S(1)}, u32[]{:S(2)}, u32[]{:S(2)}) collective-permute-start(bf16[4,264,512]{2,1,0:T(8,128)(2,1)S(1)} %pad_maximum_fusion.refs_1_), channel_id=1, source_target_pairs={{0,8},{1,3},{2,10},{3,1},{4,12},{5,7},{6,14},{7,5},{8,0},{9,11},{1... | collective-permute-start | bytes 3244040 | tf_op jit(solution)/shard_map/ppermute | solution.py:254
  26.5 28.9 %collective-permute-start.4 = (bf16[4,264,512]{2,1,0:T(8,128)(2,1)S(1)}, bf16[4,264,512]{2,1,0:T(8,128)(2,1)}, u32[]{:S(2)}, u32[]{:S(2)}) collective-permute-start(bf16[4,264,512]{2,1,0:T(8,128)(2,1)S(1)} %pad_maximum_fusion.refs_1_), channel_id=1, source_target_pairs={{0,24},{1,7},{2,26},{3,5},{4,28},{5,3},{6,30},{7,1},{8,16},{9,15},... | collective-permute-start | bytes 3244040 | tf_op jit(solution)/shard_map/ppermute | solution.py:254
  29.0 8.3 %collective-permute-start.5 = (bf16[264,512]{1,0:T(8,128)(2,1)S(1)}, bf16[264,512]{1,0:T(8,128)(2,1)S(1)}, u32[]{:S(2)}, u32[]{:S(2)}) collective-permute-start(bf16[264,512]{1,0:T(8,128)(2,1)S(1)} %copy-done), channel_id=1, source_target_pairs={{0,1},{1,0},{2,3},{3,2},{4,5},{5,4},{6,7},{7,6},{8,9},{9,8},{10,11... | collective-permute-start | bytes 811016 | tf_op jit(solution)/shard_map/ppermute | solution.py:258
  38.2 16.0 %collective-permute-start.6 = (bf16[2,264,512]{2,1,0:T(8,128)(2,1)}, bf16[2,264,512]{2,1,0:T(8,128)(2,1)S(1)}, u32[]{:S(2)}, u32[]{:S(2)}) collective-permute-start(bf16[2,264,512]{2,1,0:T(8,128)(2,1)} %pad_maximum_fusion.1), channel_id=1, source_target_pairs={{0,32},{1,481},{2,34},{3,483},{4,36},{5,485},{6,38},{7,487},{8,40}... | collective-permute-start | bytes 1622024 | tf_op jit(solution)/shard_map/ppermute | solution.py:259
  55.4 7.1 %copy-start.1 = (f32[2,128,512]{2,1,0:T(8,128)S(1)}, f32[2,128,512]{2,1,0:T(8,128)}, u32[]{:S(2)}) copy-start(f32[2,128,512]{2,1,0:T(8,128)} %rows.3) | copy-start | bytes 1572868
  58.6 3.9 %collective-permute-start.8 = (f32[2,136,512]{2,1,0:T(8,128)S(1)}, f32[2,136,512]{2,1,0:T(8,128)S(1)}, u32[]{:S(2)}, u32[]{:S(2)}) collective-permute-start(f32[2,136,512]{2,1,0:T(8,128)S(1)} %get-tuple-element.16), channel_id=1, source_target_pairs={{0,1},{1,0},{2,3},{3,2},{4,5},{5,4},{6,7},{7,6},{8,9},{9,8},{10,11... | collective-permute-start | bytes 1671176 | tf_op jit(solution)/shard_map/ppermute | solution.py:293

commit v2 on v1

v2 whole, which is shorter than its diff:
```python
import jax
import jax.numpy as jnp
from jax import lax
from jax.experimental import pallas as pl
from jax.experimental.pallas import tpu as pltpu
from jax.sharding import PartitionSpec as P

KO = 4
KI = 3
R = 128
E = 512
SIDE = 4
ROWS = 2 * R + 8
TOGETHER = 4

inv_band = 40.0
eps = 1e-06

f32 = jnp.float32
bf16 = jnp.bfloat16


def whole():
    return pl.BlockSpec(memory_space=pltpu.VMEM)


def scalars():
    return pl.BlockSpec(memory_space=pltpu.SMEM)


def call(kernel, out_shape, in_specs, flops, nbytes, scratch=()):
    return pl.pallas_call(
        kernel,
        out_shape=out_shape,
        in_specs=in_specs,
        scratch_shapes=scratch,
        out_specs=jax.tree.map(lambda _: whole(), out_shape),
        cost_estimate=pl.CostEstimate(flops=flops, bytes_accessed=nbytes, transcendentals=0),
        compiler_params=pltpu.CompilerParams(vmem_limit_bytes=6 << 20),
    )


def array(shape, dtype):
    return jax.ShapeDtypeStruct(shape, dtype)


def column_scale(q):
    wide = q.astype(f32)
    return lax.rsqrt(jnp.sum(wide * wide, axis=1, keepdims=True) * (1.0 / E) + eps)


def tiles(jobs, turned, scale, sums):
    weighted = []
    for q, p, times in jobs:
        inner = jnp.dot(q, turned[p], preferred_element_type=f32)
        kernel = jnp.exp(inner * column_scale(q) * scale[p, 0:1, :])
        weighted.append(kernel * times)
    pulled = [
        lax.dot_general(
            w.astype(bf16), q, (((0,), (0,)), ((), ())), preferred_element_type=f32
        )
        for (q, p, times), w in zip(jobs, weighted)
    ]
    for (q, p, times), w, rows in zip(jobs, weighted, pulled):
        sums[p, R : R + 1, :R] += jnp.sum(w, axis=0, keepdims=True)
        sums[p, :R, :] += rows


def prepare(own, other, turned, scale, asked):
    lane = lax.broadcasted_iota(jnp.int32, (1, E), 1) // R
    for n, (rows, b) in enumerate(((own, 0), (own, 1), (other, 0), (other, 1))):
        block = rows[b * R : (b + 1) * R, :]
        turned[n] = block.T
        column = column_scale(block) * (inv_band / E)
        scale[n] = jnp.broadcast_to(column, (R, R)).T[:8]
    own_names = own[2 * R :, :].astype(f32)
    other_names = other[2 * R :, :].astype(f32)
    for j in range(KI):
        asked[j : j + 1, :] = jnp.where(
            lane < 2,
            jnp.where(lane == 0, own_names[j : j + 1], own_names[4 + j : 5 + j]),
            jnp.where(lane == 2, other_names[j : j + 1], other_names[4 + j : 5 + j]),
        )


def write_job(jobs, at, *job):
    for row, value in enumerate(job):
        jobs[row, at] = value


def across_jobs(piece, upper, own, other, across, jobs, total):
    for n, rows in enumerate((own, other)):
        near_names = rows[2 * R :, :].astype(f32)
        far_names = across[n, 2 * R :, :].astype(f32)
        for b in range(2):
            row = 4 * b + KI
            ours = jnp.max(near_names[row : row + 1, :R]).astype(jnp.int32)
            named = jnp.max(far_names[row : row + 1, :R]).astype(jnp.int32)
            far = jnp.clip(jnp.where(upper, ours, b), 0, 1)
            near = jnp.clip(jnp.where(upper, b, named), 0, 1)
            write_job(jobs, total, piece, 2 * n + far, 2 * n + near, 1)
            total = total + 1
    return total


def partner(at, swap):
    near = at + 1 - 2 * (at % 2)
    away = SIDE - 1 - at
    return jnp.where(swap == 0, at, jnp.where(swap == 1, near, jnp.where(swap == 2, away, (at + 2) % SIDE)))


def inner_jobs(pieces, place, asked, jobs, total):
    dev = place[0]
    y, x, core = dev // 8, dev // 2 % SIDE, dev % 2
    lane = lax.broadcasted_iota(jnp.int32, (1, E), 1) // R
    code = jnp.where(lane < 2, dev * 2 + lane, (dev + 1 - 2 * core) * 2 + lane - 2).astype(f32)
    digits = jnp.zeros((1, E), f32)
    places = []
    for piece, rows, firsts, second in pieces:
        for k, first in enumerate(firsts):
            from_x = partner(x, jnp.where(core == 0, first, second))
            from_y = partner(y, jnp.where(core == 0, second, first))
            source = (from_y * SIDE + from_x) * 2 + core
            names = rows[k, 2 * R :, :].astype(f32)
            for b in range(2):
                block = (source * 2 + b).astype(f32)
                count = jnp.zeros((1, E), f32)
                for j in range(KI):
                    count += jnp.where(names[4 * b + j : 4 * b + j + 1] == code, 1.0, 0.0)
                    count += jnp.where(asked[j : j + 1, :] == block, 1.0, 0.0)
                digits += count * float(4 ** len(places))
                places.append((piece, 2 * k + b))
    for p in range(4):
        word = jnp.max(digits[:, p * R : (p + 1) * R]).astype(jnp.int32)
        for n, (piece, block) in enumerate(places):
            times = (word >> (2 * n)) & 3
            write_job(jobs, total, piece, block, p, times)
            total = total + jnp.where(times > 0, 1, 0)
    return total


def run_jobs(far, turned, scale, sums, jobs, total, held):
    for n in range(TOGETHER - 1):
        write_job(jobs, total + n, 0, 0, 0, 0)

    def some(i, carry):
        taken = []
        for t in range(TOGETHER):
            piece, n, p, times = (jobs[row, i * TOGETHER + t] for row in range(4))
            for number, rows in enumerate(far):

                @pl.when(piece == number)
                def _():
                    held[t] = rows[n // 2, pl.ds(pl.multiple_of(n % 2 * R, R), R), :]

            taken.append((held[t], p, times.astype(f32)))
        tiles(taken, turned, scale, sums)
        return carry

    lax.fori_loop(0, (total + TOGETHER - 1) // TOGETHER, some, 0)


def first_kernel(origins, place, own, other, *refs):
    far = refs[: len(origins)]
    turned, scale, asked, sums, jobs, held = refs[len(origins) :]
    prepare(own, other, turned, scale, asked)
    sums[...] = jnp.zeros(sums.shape, f32)
    for b in range(2):
        write_job(jobs, b, 0, 1 - b, b, 2 * KO)
    total = jnp.int32(2)
    pieces = [(n, rows, *origins[n]) for n, rows in enumerate(far)]
    for n in range(0, len(pieces), 2):
        total = inner_jobs(pieces[n : n + 2], place, asked, jobs, total)
    run_jobs(far, turned, scale, sums, jobs, total, held)


def middle_kernel(origins, place, own, other, across, *refs):
    far = refs[: len(origins)]
    turned, scale, asked, sums_in, sums, jobs, held = refs[len(origins) :]
    sums[...] = sums_in[...]
    total = across_jobs(len(far), place[1] == 1, own, other, across, jobs, jnp.int32(0))
    pieces = [(n, rows, *origins[n]) for n, rows in enumerate(far)]
    for n in range(0, len(pieces), 2):
        total = inner_jobs(pieces[n : n + 2], place, asked, jobs, total)
    run_jobs((*far, across), turned, scale, sums, jobs, total, held)


def last_kernel(origins, place, *refs):
    far = refs[: len(origins)]
    turned, scale, asked, sums_in, mine, theirs, jobs, held, sums = refs[len(origins) :]
    sums[...] = sums_in[...]
    pieces = [(n, rows, *origins[n]) for n, rows in enumerate(far)]
    total = inner_jobs(pieces, place, asked, jobs, jnp.int32(0))
    run_jobs(far, turned, scale, sums, jobs, total, held)
    mine[...] = sums[:2]
    theirs[...] = sums[2:]


def finish_kernel(rows, sums, received, out):
    for b in range(2):
        degree = sums[b, R : R + 1, :R] + received[b, R : R + 1, :R]
        column = jnp.broadcast_to(0.5 / degree, (R, R)).T
        for t in range(E // R):
            at = slice(t * R, (t + 1) * R)
            pulled = sums[b, :R, at] + received[b, :R, at]
            out[b, :, at] = 0.5 * rows[b, :, at] + pulled * column


def swaps(stage, swap):
    to = {1: (1, 0, 3, 2), 2: (3, 2, 1, 0), 3: (2, 3, 0, 1)}[swap]
    pairs = []
    for y in range(SIDE):
        for x in range(SIDE):
            for core in range(2):
                along_x = (core + stage) % 2 == 0
                to_x, to_y = (to[x], y) if along_x else (x, to[y])
                pairs.append(((y * SIDE + x) * 2 + core, (to_y * SIDE + to_x) * 2 + core))
    return pairs


def across_swaps(groups, devices):
    pairs = []
    for z in range(groups):
        for dev in range(devices):
            to = (z + 1 if (z + dev) % 2 == 0 else z - 1) % groups
            pairs.append((z * devices + dev, to * devices + dev))
    return pairs


def local(embeddings, neighbours):
    groups, devices = lax.axis_size("group"), lax.axis_size("dev")
    dev = lax.axis_index("dev").astype(jnp.int32)
    upper = (lax.axis_index("group").astype(jnp.int32) + dev) % 2 == 0
    place = jnp.where(jnp.arange(2) == 0, dev, upper.astype(jnp.int32))
    names = neighbours[:, KO:]
    names = jnp.where(jnp.arange(KI + 1) < KI, names % (2 * devices), names % 2).astype(bf16)
    packed = jnp.concatenate(
        [
            embeddings.astype(bf16).reshape(2 * R, E),
            jnp.broadcast_to(names.reshape(8, 1), (8, E)),
        ]
    )

    def along(value, stage, swap):
        return lax.ppermute(value, "dev", swaps(stage, swap))

    between = [(i, i ^ 1) for i in range(devices)]
    opposite = along(packed, 0, 3)
    one = along(packed, 0, 1)
    two = along(packed, 0, 2)
    other = lax.ppermute(packed, "dev", between)
    even = jnp.stack([packed, opposite])
    even_two = along(even, 1, 2)
    odd = jnp.stack([one, two])
    odd_one = along(odd, 1, 1)
    even_one = along(even, 1, 1)
    odd_two = along(odd, 1, 2)
    across = lax.ppermute(
        jnp.stack([packed, other]), ("group", "dev"), across_swaps(groups, devices)
    )
    even_far = along(even_two, 1, 1)
    odd_far = along(odd_one, 1, 2)

    all_sums, two_sums = array((4, R + 8, E), f32), array((2, R + 8, E), f32)

    def run(kernel, origins, out_shape, *args, scratch=()):
        def body(*refs):
            kernel(origins, *refs)

        return call(
            body,
            out_shape,
            [scalars()] + [whole()] * len(args),
            200_000_000,
            2 << 20,
            [
                pltpu.SMEM((4, 16 * len(origins) + 8 + TOGETHER), jnp.int32),
                pltpu.VMEM((TOGETHER, R, E), bf16),
                *scratch,
            ],
        )(place, *args)

    own_far, both = (0, 3), (1, 2)
    turned, scale, asked, sums = run(
        first_kernel,
        ((own_far, 0), (both, 0), (own_far, 2), (both, 1)),
        (array((4, E, R), bf16), array((4, 8, R), f32), array((8, E), f32), all_sums),
        packed, other, even, odd, even_two, odd_one,
    )
    sums = run(
        middle_kernel,
        ((own_far, 1), (both, 2)),
        all_sums,
        packed, other, across, even_one, odd_two, turned, scale, asked, sums,
    )
    sums, theirs = run(
        last_kernel,
        ((own_far, 3), (both, 3)),
        (two_sums, two_sums),
        even_far, odd_far, turned, scale, asked, sums,
        scratch=[pltpu.VMEM(all_sums.shape, f32)],
    )
    received = lax.ppermute(theirs, "dev", between)
    return call(
        finish_kernel,
        array(embeddings.shape, f32),
        [whole()] * 3,
        1 << 20,
        2 << 20,
    )(embeddings, sums, received)


def solution(mesh):
    in_specs = (P(("group", "dev"), None, None), P(("group", "dev"), None))
    out_specs = P(("group", "dev"), None, None)
    return jax.shard_map(local, mesh=mesh, in_specs=in_specs, out_specs=out_specs, check_vma=False)
```

time: 63.9 us -> 63.9 us (level)
  starting transfers between devices: 37.3 us -> 44.1 us
  waiting for transfers between devices: 12.4 us -> 6.27 us
  Pallas kernels: 11.5 us -> 9.8 us
  other arithmetic: 2.03 us -> 2.89 us
    ppermute x6 -> x9, starting transfers between devices: 19.6 us -> 24.9 us  [along(): return lax.ppermute(value, 'dev', swaps(stage, swap))]
    ppermute x1, waiting for transfers between devices: 3 us -> 0.01 us  [local(): lax.ppermute(jnp.stack([packed, other]), ('group', 'dev'), across_swaps(g...]
    ppermute x6 -> x9, waiting for transfers between devices: 6.32 us -> 4.34 us  [along(): return lax.ppermute(value, 'dev', swaps(stage, swap))]
    convert_element_type x0 -> x2, other arithmetic: none -> 1.84 us  [the longest x1 1.07 us: local(): embeddings.astype(bf16).reshape(2 * R, E)]
    pallas_call x6 -> x3, Pallas kernels: 10.6 us -> 8.82 us  [run(): call(body, out_shape, [scalars()] + [whole()] * len(args), 200000000, 2 <...]
    ppermute x1, starting transfers between devices: 7.14 us -> 8.79 us  [local(): other = lax.ppermute(packed, 'dev', between)]
    ppermute x1, waiting for transfers between devices: 1.15 us -> 0.01 us  [local(): other = lax.ppermute(packed, 'dev', between)]
    another operation x1, other arithmetic: 1.16 us -> 0.05 us  [local(): odd = jnp.stack([one, two])]
  transfers between devices with their start and end apart: 9 -> 12, of which waited for: 5 -> 3; matrix products, arithmetic and copies ran while one was open for 1% -> 1% of each run, Pallas kernels for 9% -> 9%
where the time goes in v2:
time: 63.9 us; the launch traced here: 63.4 us
  starting transfers between devices  44.1 us (69%)
  Pallas kernels  9.8 us (15%)
  waiting for transfers between devices  6.27 us (10%)
  other arithmetic  2.89 us (5%)
    ppermute x9, starting transfers between devices, along(): return lax.ppermute(value, 'dev', swaps(stage, swap))  24.9 us
    pallas_call x3, Pallas kernels, run(): call(body, out_shape, [scalars()] + [whole()] * len(args), 200000000, 2 <...  8.82 us
    ppermute x1, starting transfers between devices, local(): other = lax.ppermute(packed, 'dev', between)  8.79 us
    ppermute x1, starting transfers between devices, local(): lax.ppermute(jnp.stack([packed, other]), ('group', 'dev'), across_swaps(g...  8.47 us
    ppermute x9, waiting for transfers between devices, along(): return lax.ppermute(value, 'dev', swaps(stage, swap))  4.34 us
    ppermute x1, waiting for transfers between devices, local(): received = lax.ppermute(theirs, 'dev', between)  1.92 us
    ppermute x1, starting transfers between devices, local(): received = lax.ppermute(theirs, 'dev', between)  1.92 us
  transfers between devices with their start and end apart: 12, of which 3 were waited for; matrix products, arithmetic and copies ran while one was open for 1% of the time, Pallas kernels for 9%

profile of v2, /device:TPU:1, one launch (start us, length us, event | category | flops | bytes accessed | tf_op | source)
XLA Modules:
  0.0 63.4 jit_solution(772830010258788611)
XLA Ops:
  0.0 1.1 %convert_element_type.10 = bf16[2,128,512]{2,1,0:T(8,128)(2,1)S(1)} convert(f32[2,128,512]{2,1,0:T(8,128)} %rows.1) | non-fusion elementwise | flops 131072 | bytes 786432 | tf_op jit(solution)/shard_map/convert_element_type | solution.py:239
  1.1 0.8 %fusion.1 = bf16[2,4]{1,0:T(2,128)(2,1)S(1)} fusion(s32[2,8]{1,0:T(2,128)} %param.3, pred[4]{0:T(512)(128)(4,1)S(1)} %iota_compare_fusion), kind=kLoop, calls=%fused_computation.11 | loop fusion | flops 168 | bytes 52 | tf_op jit(solution)/shard_map/convert_element_type | solution.py:236
  1.8 0.1 reshape.6
  1.9 0.1 pad_maximum_fusion.3
  2.1 8.8 %collective-permute-start.7 = (bf16[264,512]{1,0:T(8,128)(2,1)S(1)}, bf16[264,512]{1,0:T(8,128)(2,1)S(1)}, u32[]{:S(2)}, u32[]{:S(2)}) collective-permute-start(bf16[264,512]{1,0:T(8,128)(2,1)S(1)} %get-tuple-element.19.refs_1_), channel_id=1, source_target_pairs={{0,1},{1,0},{2,3},{3,2},{4,5},{5,4},{6,7},{7,6},{8,9},{9,8},{10,11... | collective-permute-start | bytes 811016 | tf_op jit(solution)/shard_map/ppermute | solution.py:251
  10.9 1.9 %collective-permute-start = (bf16[264,512]{1,0:T(8,128)(2,1)S(1)}, bf16[264,512]{1,0:T(8,128)(2,1)S(1)}, u32[]{:S(2)}, u32[]{:S(2)}) collective-permute-start(bf16[264,512]{1,0:T(8,128)(2,1)S(1)} %get-tuple-element.19.refs_1_), channel_id=1, source_target_pairs={{0,4},{1,17},{2,6},{3,19},{4,0},{5,21},{6,2},{7,23},{8,12},{9,25},... | collective-permute-start | bytes 811016 | tf_op jit(solution)/shard_map/ppermute | solution.py:245
  12.8 1.9 %collective-permute-start.3 = (bf16[264,512]{1,0:T(8,128)(2,1)S(1)}, bf16[264,512]{1,0:T(8,128)(2,1)S(1)}, u32[]{:S(2)}, u32[]{:S(2)}) collective-permute-start(bf16[264,512]{1,0:T(8,128)(2,1)S(1)} %get-tuple-element.19.refs_1_), channel_id=1, source_target_pairs={{0,2},{1,9},{2,0},{3,11},{4,6},{5,13},{6,4},{7,15},{8,10},{9,1},{1... | collective-permute-start | bytes 811016 | tf_op jit(solution)/shard_map/ppermute | solution.py:245
  14.7 5.1 %collective-permute-start.4 = (bf16[264,512]{1,0:T(8,128)(2,1)S(1)}, bf16[264,512]{1,0:T(8,128)(2,1)S(1)}, u32[]{:S(2)}, u32[]{:S(2)}) collective-permute-start(bf16[264,512]{1,0:T(8,128)(2,1)S(1)} %get-tuple-element.19.refs_1_), channel_id=1, source_target_pairs={{0,6},{1,25},{2,4},{3,27},{4,2},{5,29},{6,0},{7,31},{8,14},{9,17},... | collective-permute-start | bytes 811016 | tf_op jit(solution)/shard_map/ppermute | solution.py:245
  19.9 0.0 collective-permute-done.7.refs_2_
  19.9 0.0 collective-permute-done
  19.9 0.9 %pad_maximum_fusion = (bf16[2,264,512]{2,1,0:T(8,128)(2,1)}, bf16[2,264,512]{2,1,0:T(8,128)(2,1)S(1)}) fusion(bf16[1,264,512]{2,1,0:T(8,128)(2,1)S(1)} %get-tuple-element.20, bf16[1,264,512]{2,1,0:T(8,128)(2,1)S(1)} %bitcast.7, bf16[1,264,512]{2,1,0:T(8,128)(2,1)S(1)} %bitcast.11), kind=kLoop, calls=%fused_computation | loop fusion | flops 540672 | bytes 1892352 | tf_op jit(solution)/shard_map/stack | solution.py:259
  20.8 1.9 %collective-permute-start.1 = (bf16[2,264,512]{2,1,0:T(8,128)(2,1)S(1)}, bf16[2,264,512]{2,1,0:T(8,128)(2,1)}, u32[]{:S(2)}, u32[]{:S(2)}) collective-permute-start(bf16[2,264,512]{2,1,0:T(8,128)(2,1)S(1)} %get-tuple-element.18.refs_3_), channel_id=1, source_target_pairs={{0,24},{1,7},{2,26},{3,5},{4,28},{5,3},{6,30},{7,1},{8,16},{9,15},... | collective-permute-start | bytes 1622024 | tf_op jit(solution)/shard_map/ppermute | solution.py:245
  22.7 1.3 %collective-permute-done.4 = bf16[264,512]{1,0:T(8,128)(2,1)S(1)} collective-permute-done((bf16[264,512]{1,0:T(8,128)(2,1)S(1)}, bf16[264,512]{1,0:T(8,128)(2,1)S(1)}, u32[]{:S(2)}, u32[]{:S(2)}) %collective-permute-start.4) | collective-permute-done | bytes 270368 | tf_op jit(solution)/shard_map/ppermute | solution.py:245
  24.0 0.1 pad_maximum_fusion.2.refs_4_
  24.0 1.9 %collective-permute-start.5 = (bf16[2,264,512]{2,1,0:T(8,128)(2,1)S(1)}, bf16[2,264,512]{2,1,0:T(8,128)(2,1)}, u32[]{:S(2)}, u32[]{:S(2)}) collective-permute-start(bf16[2,264,512]{2,1,0:T(8,128)(2,1)S(1)} %pad_maximum_fusion.2.refs_4_), channel_id=1, source_target_pairs={{0,8},{1,3},{2,10},{3,1},{4,12},{5,7},{6,14},{7,5},{8,0},{9,11},{1... | collective-permute-start | bytes 1622024 | tf_op jit(solution)/shard_map/ppermute | solution.py:245
  26.0 3.4 %collective-permute-start.9 = (bf16[2,264,512]{2,1,0:T(8,128)(2,1)S(1)}, bf16[2,264,512]{2,1,0:T(8,128)(2,1)S(1)}, u32[]{:S(2)}, u32[]{:S(2)}) collective-permute-start(bf16[2,264,512]{2,1,0:T(8,128)(2,1)S(1)} %get-tuple-element.18.refs_3_), channel_id=1, source_target_pairs={{0,8},{1,3},{2,10},{3,1},{4,12},{5,7},{6,14},{7,5},{8,0},{9,11},{1... | collective-permute-start | bytes 1622024 | tf_op jit(solution)/shard_map/ppermute | solution.py:245
  29.3 8.5 %collective-permute-start.8 = (bf16[2,264,512]{2,1,0:T(8,128)(2,1)}, bf16[2,264,512]{2,1,0:T(8,128)(2,1)S(1)}, u32[]{:S(2)}, u32[]{:S(2)}) collective-permute-start(bf16[2,264,512]{2,1,0:T(8,128)(2,1)} %get-tuple-element.17), channel_id=1, source_target_pairs={{0,32},{1,481},{2,34},{3,483},{4,36},{5,485},{6,38},{7,487},{8,40}... | collective-permute-start | bytes 1622024 | tf_op jit(solution)/shard_map/ppermute | solution.py:258
  37.8 4.1 %collective-permute-start.10 = (bf16[2,264,512]{2,1,0:T(8,128)(2,1)S(1)}, bf16[2,264,512]{2,1,0:T(8,128)(2,1)S(1)}, u32[]{:S(2)}, u32[]{:S(2)}) collective-permute-start(bf16[2,264,512]{2,1,0:T(8,128)(2,1)S(1)} %pad_maximum_fusion.2.refs_4_), channel_id=1, source_target_pairs={{0,24},{1,7},{2,26},{3,5},{4,28},{5,3},{6,30},{7,1},{8,16},{9,15},... | collective-permute-start | bytes 1622024 | tf_op jit(solution)/shard_map/ppermute | solution.py:245
  41.9 0.0 collective-permute-done.1.refs_5_
  41.9 1.9 %collective-permute-start.2 = (bf16[2,264,512]{2,1,0:T(8,128)(2,1)}, bf16[2,264,512]{2,1,0:T(8,128)(2,1)}, u32[]{:S(2)}, u32[]{:S(2)}) collective-permute-start(bf16[2,264,512]{2,1,0:T(8,128)(2,1)} %collective-permute-done.1.refs_5_), channel_id=1, source_target_pairs={{0,8},{1,3},{2,10},{3,1},{4,12},{5,7},{6,14},{7,5},{8,0},{9,11},{1... | collective-permute-start | bytes 1622024 | tf_op jit(solution)/shard_map/ppermute | solution.py:245
  43.9 0.0 collective-permute-done.5.refs_6_
  43.9 2.7 %collective-permute-start.6 = (bf16[2,264,512]{2,1,0:T(8,128)(2,1)}, bf16[2,264,512]{2,1,0:T(8,128)(2,1)}, u32[]{:S(2)}, u32[]{:S(2)}) collective-permute-start(bf16[2,264,512]{2,1,0:T(8,128)(2,1)} %collective-permute-done.5.refs_6_), channel_id=1, source_target_pairs={{0,24},{1,7},{2,26},{3,5},{4,28},{5,3},{6,30},{7,1},{8,16},{9,15},... | collective-permute-start | bytes 1622024 | tf_op jit(solution)/shard_map/ppermute | solution.py:245
  46.6 3.5 %shard_map.28 = (bf16[4,512,128]{2,1,0:T(8,128)(2,1)S(1)}, f32[4,8,128]{2,1,0:T(8,128)S(1)}, f32[8,512]{1,0:T(8,128)S(1)}, f32[4,136,512]{2,1,0:T(8,128)S(1)}) custom-call(s32[2]{0:T(128)S(1)} %compare_select_fusion.refs_0_, bf16[264,512]{1,0:T(8,128)(2,1)S(1)} %get-tuple-element.19.refs_1_, bf16[264,512]{1,0:T(8,128)(2,1)S(1)} %collective-permute-done.7.refs_2_, ...), custom_call_target="tpu_custom_call" | custom-call | flops 200000000 | bytes 2097152 | tf_op jit(solution)/shard_map/pallas_call | solution.py:270
  50.1 0.0 collective-permute-done.8.refs_3_
  50.1 2.3 %shard_map.29.refs_6_ = f32[4,136,512]{2,1,0:T(8,128)S(1)} custom-call(s32[2]{0:T(128)S(1)} %compare_select_fusion.refs_0_, bf16[264,512]{1,0:T(8,128)(2,1)S(1)} %get-tuple-element.19.refs_1_, bf16[264,512]{1,0:T(8,128)(2,1)S(1)} %collective-permute-done.7.refs_2_, bf16[2,264,512]{2,1,0:T(8,128)(2,1)S(1)} %collective-permute-done.8.refs_3_, ...), custom_call_target="tpu_custom_call" | custom-call | flops 200000000 | bytes 2097152 | tf_op jit(solution)/shard_map/pallas_call | solution.py:270
  52.5 0.0 copy-start
  52.5 0.0 collective-permute-done.2.refs_1_
  52.5 3.0 %collective-permute-done.6.refs_2_ = bf16[2,264,512]{2,1,0:T(8,128)(2,1)} collective-permute-done((bf16[2,264,512]{2,1,0:T(8,128)(2,1)}, bf16[2,264,512]{2,1,0:T(8,128)(2,1)}, u32[]{:S(2)}, u32[]{:S(2)}) %collective-permute-start.6) | collective-permute-done | bytes 540704 | tf_op jit(solution)/shard_map/ppermute | solution.py:245
  55.5 3.0 %shard_map.30 = (f32[2,136,512]{2,1,0:T(8,128)S(1)}, f32[2,136,512]{2,1,0:T(8,128)S(1)}) custom-call(s32[2]{0:T(128)S(1)} %compare_select_fusion.refs_0_, bf16[2,264,512]{2,1,0:T(8,128)(2,1)} %collective-permute-done.2.refs_1_, bf16[2,264,512]{2,1,0:T(8,128)(2,1)} %collective-permute-done.6.refs_2_, ...), custom_call_target="tpu_custom_call" | custom-call | flops 200000000 | bytes 2097152 | tf_op jit(solution)/shard_map/pallas_call | solution.py:270
  58.5 1.9 %collective-permute-start.11 = (f32[2,136,512]{2,1,0:T(8,128)S(1)}, f32[2,136,512]{2,1,0:T(8,128)S(1)}, u32[]{:S(2)}, u32[]{:S(2)}) collective-permute-start(f32[2,136,512]{2,1,0:T(8,128)S(1)} %get-tuple-element.16), channel_id=1, source_target_pairs={{0,1},{1,0},{2,3},{3,2},{4,5},{5,4},{6,7},{7,6},{8,9},{9,8},{10,11... | collective-permute-start | bytes 1671176 | tf_op jit(solution)/shard_map/ppermute | solution.py:303
  60.4 1.9 %collective-permute-done.11.received = f32[2,136,512]{2,1,0:T(8,128)S(1)} collective-permute-done((f32[2,136,512]{2,1,0:T(8,128)S(1)}, f32[2,136,512]{2,1,0:T(8,128)S(1)}, u32[]{:S(2)}, u32[]{:S(2)}) %collective-permute-start.11) | collective-permute-done | bytes 557088 | tf_op jit(solution)/shard_map/ppermute | solution.py:303
  62.4 1.0 %shard_map.31 = f32[2,128,512]{2,1,0:T(8,128)} custom-call(f32[2,128,512]{2,1,0:T(8,128)S(1)} %copy-done, f32[2,136,512]{2,1,0:T(8,128)S(1)} %get-tuple-element.15.sums, f32[2,136,512]{2,1,0:T(8,128)S(1)} %collective-permute-done.11.received), custom_call_target="tpu_custom_call" | custom-call | flops 1048576 | bytes 2097152 | tf_op jit(solution)/shard_map/pallas_call | solution.py:304
  (7 shorter events, 0.0 us)
Async XLA Ops:
  2.1 17.8 %collective-permute-start.7 = (bf16[264,512]{1,0:T(8,128)(2,1)S(1)}, bf16[264,512]{1,0:T(8,128)(2,1)S(1)}, u32[]{:S(2)}, u32[]{:S(2)}) collective-permute-start(bf16[264,512]{1,0:T(8,128)(2,1)S(1)} %get-tuple-element.19.refs_1_), channel_id=1, source_target_pairs={{0,1},{1,0},{2,3},{3,2},{4,5},{5,4},{6,7},{7,6},{8,9},{9,8},{10,11... | collective-permute-start | bytes 811016 | tf_op jit(solution)/shard_map/ppermute | solution.py:251
  10.9 9.0 %collective-permute-start = (bf16[264,512]{1,0:T(8,128)(2,1)S(1)}, bf16[264,512]{1,0:T(8,128)(2,1)S(1)}, u32[]{:S(2)}, u32[]{:S(2)}) collective-permute-start(bf16[264,512]{1,0:T(8,128)(2,1)S(1)} %get-tuple-element.19.refs_1_), channel_id=1, source_target_pairs={{0,4},{1,17},{2,6},{3,19},{4,0},{5,21},{6,2},{7,23},{8,12},{9,25},... | collective-permute-start | bytes 811016 | tf_op jit(solution)/shard_map/ppermute | solution.py:245
  12.8 9.9 %collective-permute-start.3 = (bf16[264,512]{1,0:T(8,128)(2,1)S(1)}, bf16[264,512]{1,0:T(8,128)(2,1)S(1)}, u32[]{:S(2)}, u32[]{:S(2)}) collective-permute-start(bf16[264,512]{1,0:T(8,128)(2,1)S(1)} %get-tuple-element.19.refs_1_), channel_id=1, source_target_pairs={{0,2},{1,9},{2,0},{3,11},{4,6},{5,13},{6,4},{7,15},{8,10},{9,1},{1... | collective-permute-start | bytes 811016 | tf_op jit(solution)/shard_map/ppermute | solution.py:245
  14.7 9.3 %collective-permute-start.4 = (bf16[264,512]{1,0:T(8,128)(2,1)S(1)}, bf16[264,512]{1,0:T(8,128)(2,1)S(1)}, u32[]{:S(2)}, u32[]{:S(2)}) collective-permute-start(bf16[264,512]{1,0:T(8,128)(2,1)S(1)} %get-tuple-element.19.refs_1_), channel_id=1, source_target_pairs={{0,6},{1,25},{2,4},{3,27},{4,2},{5,29},{6,0},{7,31},{8,14},{9,17},... | collective-permute-start | bytes 811016 | tf_op jit(solution)/shard_map/ppermute | solution.py:245
  20.8 21.2 %collective-permute-start.1 = (bf16[2,264,512]{2,1,0:T(8,128)(2,1)S(1)}, bf16[2,264,512]{2,1,0:T(8,128)(2,1)}, u32[]{:S(2)}, u32[]{:S(2)}) collective-permute-start(bf16[2,264,512]{2,1,0:T(8,128)(2,1)S(1)} %get-tuple-element.18.refs_3_), channel_id=1, source_target_pairs={{0,24},{1,7},{2,26},{3,5},{4,28},{5,3},{6,30},{7,1},{8,16},{9,15},... | collective-permute-start | bytes 1622024 | tf_op jit(solution)/shard_map/ppermute | solution.py:245
  24.0 19.8 %collective-permute-start.5 = (bf16[2,264,512]{2,1,0:T(8,128)(2,1)S(1)}, bf16[2,264,512]{2,1,0:T(8,128)(2,1)}, u32[]{:S(2)}, u32[]{:S(2)}) collective-permute-start(bf16[2,264,512]{2,1,0:T(8,128)(2,1)S(1)} %pad_maximum_fusion.2.refs_4_), channel_id=1, source_target_pairs={{0,8},{1,3},{2,10},{3,1},{4,12},{5,7},{6,14},{7,5},{8,0},{9,11},{1... | collective-permute-start | bytes 1622024 | tf_op jit(solution)/shard_map/ppermute | solution.py:245
  26.0 24.1 %collective-permute-start.9 = (bf16[2,264,512]{2,1,0:T(8,128)(2,1)S(1)}, bf16[2,264,512]{2,1,0:T(8,128)(2,1)S(1)}, u32[]{:S(2)}, u32[]{:S(2)}) collective-permute-start(bf16[2,264,512]{2,1,0:T(8,128)(2,1)S(1)} %get-tuple-element.18.refs_3_), channel_id=1, source_target_pairs={{0,8},{1,3},{2,10},{3,1},{4,12},{5,7},{6,14},{7,5},{8,0},{9,11},{1... | collective-permute-start | bytes 1622024 | tf_op jit(solution)/shard_map/ppermute | solution.py:245
  29.3 20.8 %collective-permute-start.8 = (bf16[2,264,512]{2,1,0:T(8,128)(2,1)}, bf16[2,264,512]{2,1,0:T(8,128)(2,1)S(1)}, u32[]{:S(2)}, u32[]{:S(2)}) collective-permute-start(bf16[2,264,512]{2,1,0:T(8,128)(2,1)} %get-tuple-element.17), channel_id=1, source_target_pairs={{0,32},{1,481},{2,34},{3,483},{4,36},{5,485},{6,38},{7,487},{8,40}... | collective-permute-start | bytes 1622024 | tf_op jit(solution)/shard_map/ppermute | solution.py:258
  37.8 12.3 %collective-permute-start.10 = (bf16[2,264,512]{2,1,0:T(8,128)(2,1)S(1)}, bf16[2,264,512]{2,1,0:T(8,128)(2,1)S(1)}, u32[]{:S(2)}, u32[]{:S(2)}) collective-permute-start(bf16[2,264,512]{2,1,0:T(8,128)(2,1)S(1)} %pad_maximum_fusion.2.refs_4_), channel_id=1, source_target_pairs={{0,24},{1,7},{2,26},{3,5},{4,28},{5,3},{6,30},{7,1},{8,16},{9,15},... | collective-permute-start | bytes 1622024 | tf_op jit(solution)/shard_map/ppermute | solution.py:245
  41.9 10.6 %collective-permute-start.2 = (bf16[2,264,512]{2,1,0:T(8,128)(2,1)}, bf16[2,264,512]{2,1,0:T(8,128)(2,1)}, u32[]{:S(2)}, u32[]{:S(2)}) collective-permute-start(bf16[2,264,512]{2,1,0:T(8,128)(2,1)} %collective-permute-done.1.refs_5_), channel_id=1, source_target_pairs={{0,8},{1,3},{2,10},{3,1},{4,12},{5,7},{6,14},{7,5},{8,0},{9,11},{1... | collective-permute-start | bytes 1622024 | tf_op jit(solution)/shard_map/ppermute | solution.py:245
  43.9 11.6 %collective-permute-start.6 = (bf16[2,264,512]{2,1,0:T(8,128)(2,1)}, bf16[2,264,512]{2,1,0:T(8,128)(2,1)}, u32[]{:S(2)}, u32[]{:S(2)}) collective-permute-start(bf16[2,264,512]{2,1,0:T(8,128)(2,1)} %collective-permute-done.5.refs_6_), channel_id=1, source_target_pairs={{0,24},{1,7},{2,26},{3,5},{4,28},{5,3},{6,30},{7,1},{8,16},{9,15},... | collective-permute-start | bytes 1622024 | tf_op jit(solution)/shard_map/ppermute | solution.py:245
  52.5 9.9 %copy-start = (f32[2,128,512]{2,1,0:T(8,128)S(1)}, f32[2,128,512]{2,1,0:T(8,128)}, u32[]{:S(2)}) copy-start(f32[2,128,512]{2,1,0:T(8,128)} %rows.1) | copy-start | bytes 1572868
  58.5 3.9 %collective-permute-start.11 = (f32[2,136,512]{2,1,0:T(8,128)S(1)}, f32[2,136,512]{2,1,0:T(8,128)S(1)}, u32[]{:S(2)}, u32[]{:S(2)}) collective-permute-start(f32[2,136,512]{2,1,0:T(8,128)S(1)} %get-tuple-element.16), channel_id=1, source_target_pairs={{0,1},{1,0},{2,3},{3,2},{4,5},{5,4},{6,7},{7,6},{8,9},{9,8},{10,11... | collective-permute-start | bytes 1671176 | tf_op jit(solution)/shard_map/ppermute | solution.py:303

commit v3 on v2

--- a/solution.py
+++ b/solution.py
@@ -256,8 +256,8 @@
     even_one = along(even, 1, 1)
     odd_two = along(odd, 1, 2)
     across = lax.ppermute(
-        jnp.stack([packed, other]), ("group", "dev"), across_swaps(groups, devices)
-    )
+        jnp.concatenate([packed, other]), ("group", "dev"), across_swaps(groups, devices)
+    ).reshape(2, ROWS, E)
     even_far = along(even_two, 1, 1)
     odd_far = along(odd_one, 1, 2)
 

time: 63.9 us -> 66.6 us (1.042)
  starting transfers between devices: 44.1 us -> 46.9 us
    ppermute x9, starting transfers between devices: 24.9 us -> 31.5 us  [along(): return lax.ppermute(value, 'dev', swaps(stage, swap))]
    ppermute x1, starting transfers between devices: 8.79 us -> 6.48 us  [local(): other = lax.ppermute(packed, 'dev', between)]
    ppermute x1, starting transfers between devices: 8.47 us -> 6.99 us  [local(): lax.ppermute(jnp.concatenate([packed, other]), ('group', 'dev'), across_s...]
    another operation x1 -> x2, other arithmetic: 0.88 us -> 0.09 us  [local(): even = jnp.stack([packed, opposite])]
    concatenate x1, other arithmetic: 0.11 us -> 0.84 us  [local(): jnp.concatenate([packed, other])]
  transfers between devices with their start and end apart: 12 -> 12, of which waited for: 3 -> 4; matrix products, arithmetic and copies ran while one was open for 1% -> 1% of each run, Pallas kernels for 9% -> 9%
where the time goes in v3:
time: 66.6 us; the launch traced here: 66.4 us
  starting transfers between devices  46.9 us (70%)
  Pallas kernels  9.81 us (15%)
  waiting for transfers between devices  6.55 us (10%)
  other arithmetic  2.82 us (4%)
    ppermute x9, starting transfers between devices, along(): return lax.ppermute(value, 'dev', swaps(stage, swap))  31.5 us
    pallas_call x3, Pallas kernels, run(): call(body, out_shape, [scalars()] + [whole()] * len(args), 200000000, 2 <...  8.83 us
    ppermute x1, starting transfers between devices, local(): lax.ppermute(jnp.concatenate([packed, other]), ('group', 'dev'), across_s...  6.99 us
    ppermute x1, starting transfers between devices, local(): other = lax.ppermute(packed, 'dev', between)  6.48 us
    ppermute x9, waiting for transfers between devices, along(): return lax.ppermute(value, 'dev', swaps(stage, swap))  4.62 us
    ppermute x1, waiting for transfers between devices, local(): received = lax.ppermute(theirs, 'dev', between)  1.92 us
    ppermute x1, starting transfers between devices, local(): received = lax.ppermute(theirs, 'dev', between)  1.92 us
  transfers between devices with their start and end apart: 12, of which 4 were waited for; matrix products, arithmetic and copies ran while one was open for 1% of the time, Pallas kernels for 9%

profile of v3, /device:TPU:1, one launch (start us, length us, event | category | flops | bytes accessed | tf_op | source)
XLA Modules:
  0.0 66.4 jit_solution(3609470702052599473)
XLA Ops:
  0.0 1.1 %convert_element_type.10 = bf16[2,128,512]{2,1,0:T(8,128)(2,1)S(1)} convert(f32[2,128,512]{2,1,0:T(8,128)} %rows.1) | non-fusion elementwise | flops 131072 | bytes 786432 | tf_op jit(solution)/shard_map/convert_element_type | solution.py:239
  1.1 0.8 %fusion.1 = bf16[2,4]{1,0:T(2,128)(2,1)S(1)} fusion(s32[2,8]{1,0:T(2,128)} %param.3, pred[4]{0:T(512)(128)(4,1)S(1)} %iota_compare_fusion), kind=kLoop, calls=%fused_computation.11 | loop fusion | flops 168 | bytes 52 | tf_op jit(solution)/shard_map/convert_element_type | solution.py:236
  1.8 0.1 broadcast_in_dim.22
  1.9 0.1 broadcast_in_dim.23
  2.0 4.0 %collective-permute-start.3 = (bf16[264,512]{1,0:T(8,128)(2,1)S(1)}, bf16[264,512]{1,0:T(8,128)(2,1)S(1)}, u32[]{:S(2)}, u32[]{:S(2)}) collective-permute-start(bf16[264,512]{1,0:T(8,128)(2,1)S(1)} %get-tuple-element.18.refs_1_), channel_id=1, source_target_pairs={{0,2},{1,9},{2,0},{3,11},{4,6},{5,13},{6,4},{7,15},{8,10},{9,1},{1... | collective-permute-start | bytes 811016 | tf_op jit(solution)/shard_map/ppermute | solution.py:245
  6.1 3.8 %collective-permute-start.4 = (bf16[264,512]{1,0:T(8,128)(2,1)S(1)}, bf16[264,512]{1,0:T(8,128)(2,1)S(1)}, u32[]{:S(2)}, u32[]{:S(2)}) collective-permute-start(bf16[264,512]{1,0:T(8,128)(2,1)S(1)} %get-tuple-element.18.refs_1_), channel_id=1, source_target_pairs={{0,6},{1,25},{2,4},{3,27},{4,2},{5,29},{6,0},{7,31},{8,14},{9,17},... | collective-permute-start | bytes 811016 | tf_op jit(solution)/shard_map/ppermute | solution.py:245
  9.9 2.6 %collective-permute-start = (bf16[264,512]{1,0:T(8,128)(2,1)S(1)}, bf16[264,512]{1,0:T(8,128)(2,1)S(1)}, u32[]{:S(2)}, u32[]{:S(2)}) collective-permute-start(bf16[264,512]{1,0:T(8,128)(2,1)S(1)} %get-tuple-element.18.refs_1_), channel_id=1, source_target_pairs={{0,4},{1,17},{2,6},{3,19},{4,0},{5,21},{6,2},{7,23},{8,12},{9,25},... | collective-permute-start | bytes 811016 | tf_op jit(solution)/shard_map/ppermute | solution.py:245
  12.6 0.0 collective-permute-done.3
  12.6 1.9 %collective-permute-done.4 = bf16[264,512]{1,0:T(8,128)(2,1)S(1)} collective-permute-done((bf16[264,512]{1,0:T(8,128)(2,1)S(1)}, bf16[264,512]{1,0:T(8,128)(2,1)S(1)}, u32[]{:S(2)}, u32[]{:S(2)}) %collective-permute-start.4) | collective-permute-done | bytes 270368 | tf_op jit(solution)/shard_map/ppermute | solution.py:245
  14.5 0.1 pad_maximum_fusion.1.refs_4_
  14.6 3.1 %collective-permute-start.5 = (bf16[2,264,512]{2,1,0:T(8,128)(2,1)S(1)}, bf16[2,264,512]{2,1,0:T(8,128)(2,1)}, u32[]{:S(2)}, u32[]{:S(2)}) collective-permute-start(bf16[2,264,512]{2,1,0:T(8,128)(2,1)S(1)} %pad_maximum_fusion.1.refs_4_), channel_id=1, source_target_pairs={{0,8},{1,3},{2,10},{3,1},{4,12},{5,7},{6,14},{7,5},{8,0},{9,11},{1... | collective-permute-start | bytes 1622024 | tf_op jit(solution)/shard_map/ppermute | solution.py:245
  17.7 0.9 %collective-permute-done = bf16[264,512]{1,0:T(8,128)(2,1)S(1)} collective-permute-done((bf16[264,512]{1,0:T(8,128)(2,1)S(1)}, bf16[264,512]{1,0:T(8,128)(2,1)S(1)}, u32[]{:S(2)}, u32[]{:S(2)}) %collective-permute-start) | collective-permute-done | bytes 270368 | tf_op jit(solution)/shard_map/ppermute | solution.py:245
  18.6 0.1 pad_maximum_fusion.refs_3_
  18.7 4.4 %collective-permute-start.1 = (bf16[2,264,512]{2,1,0:T(8,128)(2,1)S(1)}, bf16[2,264,512]{2,1,0:T(8,128)(2,1)}, u32[]{:S(2)}, u32[]{:S(2)}) collective-permute-start(bf16[2,264,512]{2,1,0:T(8,128)(2,1)S(1)} %pad_maximum_fusion.refs_3_), channel_id=1, source_target_pairs={{0,24},{1,7},{2,26},{3,5},{4,28},{5,3},{6,30},{7,1},{8,16},{9,15},... | collective-permute-start | bytes 1622024 | tf_op jit(solution)/shard_map/ppermute | solution.py:245
  23.1 6.5 %collective-permute-start.7 = (bf16[264,512]{1,0:T(8,128)(2,1)S(1)}, bf16[264,512]{1,0:T(8,128)(2,1)S(1)}, u32[]{:S(2)}, u32[]{:S(2)}) collective-permute-start(bf16[264,512]{1,0:T(8,128)(2,1)S(1)} %get-tuple-element.18.refs_1_), channel_id=1, source_target_pairs={{0,1},{1,0},{2,3},{3,2},{4,5},{5,4},{6,7},{7,6},{8,9},{9,8},{10,11... | collective-permute-start | bytes 811016 | tf_op jit(solution)/shard_map/ppermute | solution.py:251
  29.6 4.7 %collective-permute-start.10 = (bf16[2,264,512]{2,1,0:T(8,128)(2,1)S(1)}, bf16[2,264,512]{2,1,0:T(8,128)(2,1)S(1)}, u32[]{:S(2)}, u32[]{:S(2)}) collective-permute-start(bf16[2,264,512]{2,1,0:T(8,128)(2,1)S(1)} %pad_maximum_fusion.1.refs_4_), channel_id=1, source_target_pairs={{0,24},{1,7},{2,26},{3,5},{4,28},{5,3},{6,30},{7,1},{8,16},{9,15},... | collective-permute-start | bytes 1622024 | tf_op jit(solution)/shard_map/ppermute | solution.py:245
  34.3 2.5 %collective-permute-start.9 = (bf16[2,264,512]{2,1,0:T(8,128)(2,1)S(1)}, bf16[2,264,512]{2,1,0:T(8,128)(2,1)S(1)}, u32[]{:S(2)}, u32[]{:S(2)}) collective-permute-start(bf16[2,264,512]{2,1,0:T(8,128)(2,1)S(1)} %pad_maximum_fusion.refs_3_), channel_id=1, source_target_pairs={{0,8},{1,3},{2,10},{3,1},{4,12},{5,7},{6,14},{7,5},{8,0},{9,11},{1... | collective-permute-start | bytes 1622024 | tf_op jit(solution)/shard_map/ppermute | solution.py:245
  36.8 0.0 collective-permute-done.7.refs_2_
  36.8 0.8 %pad_maximum_fusion.2 = bf16[528,512]{1,0:T(8,128)(2,1)} fusion(bf16[264,512]{1,0:T(8,128)(2,1)S(1)} %collective-permute-done.7.refs_2_, bf16[8,512]{1,0:T(8,128)(2,1)S(1)} %broadcast_in_dim.23, bf16[256,512]{1,0:T(8,128)(2,1)S(1)} %bitcast.9), kind=kLoop, calls=%fused_computation.2 | loop fusion | flops 1622016 | bytes 1081344 | tf_op jit(solution)/shard_map/concatenate | solution.py:259
  37.6 7.0 %collective-permute-start.8 = (bf16[528,512]{1,0:T(8,128)(2,1)}, bf16[528,512]{1,0:T(8,128)(2,1)S(1)}, u32[]{:S(2)}, u32[]{:S(2)}) collective-permute-start(bf16[528,512]{1,0:T(8,128)(2,1)} %pad_maximum_fusion.2), channel_id=1, source_target_pairs={{0,32},{1,481},{2,34},{3,483},{4,36},{5,485},{6,38},{7,487},{8,40}... | collective-permute-start | bytes 1622024 | tf_op jit(solution)/shard_map/ppermute | solution.py:258
  44.6 3.5 %collective-permute-start.6 = (bf16[2,264,512]{2,1,0:T(8,128)(2,1)}, bf16[2,264,512]{2,1,0:T(8,128)(2,1)}, u32[]{:S(2)}, u32[]{:S(2)}) collective-permute-start(bf16[2,264,512]{2,1,0:T(8,128)(2,1)} %collective-permute-done.5.refs_6_), channel_id=1, source_target_pairs={{0,24},{1,7},{2,26},{3,5},{4,28},{5,3},{6,30},{7,1},{8,16},{9,15},... | collective-permute-start | bytes 1622024 | tf_op jit(solution)/shard_map/ppermute | solution.py:245
  48.1 0.0 collective-permute-done.1.refs_5_
  48.2 2.8 %collective-permute-start.2 = (bf16[2,264,512]{2,1,0:T(8,128)(2,1)}, bf16[2,264,512]{2,1,0:T(8,128)(2,1)}, u32[]{:S(2)}, u32[]{:S(2)}) collective-permute-start(bf16[2,264,512]{2,1,0:T(8,128)(2,1)} %collective-permute-done.1.refs_5_), channel_id=1, source_target_pairs={{0,8},{1,3},{2,10},{3,1},{4,12},{5,7},{6,14},{7,5},{8,0},{9,11},{1... | collective-permute-start | bytes 1622024 | tf_op jit(solution)/shard_map/ppermute | solution.py:245
  50.9 3.5 %shard_map.28 = (bf16[4,512,128]{2,1,0:T(8,128)(2,1)S(1)}, f32[4,8,128]{2,1,0:T(8,128)S(1)}, f32[8,512]{1,0:T(8,128)S(1)}, f32[4,136,512]{2,1,0:T(8,128)S(1)}) custom-call(s32[2]{0:T(128)S(1)} %compare_select_fusion.refs_0_, bf16[264,512]{1,0:T(8,128)(2,1)S(1)} %get-tuple-element.18.refs_1_, bf16[264,512]{1,0:T(8,128)(2,1)S(1)} %collective-permute-done.7.refs_2_, ...), custom_call_target="tpu_custom_call" | custom-call | flops 200000000 | bytes 2097152 | tf_op jit(solution)/shard_map/pallas_call | solution.py:270
  54.4 0.0 collective-permute-done.9.refs_4_
  54.5 2.3 %shard_map.29.refs_6_ = f32[4,136,512]{2,1,0:T(8,128)S(1)} custom-call(s32[2]{0:T(128)S(1)} %compare_select_fusion.refs_0_, bf16[264,512]{1,0:T(8,128)(2,1)S(1)} %get-tuple-element.18.refs_1_, bf16[264,512]{1,0:T(8,128)(2,1)S(1)} %collective-permute-done.7.refs_2_, bf16[2,264,512]{2,1,0:T(8,128)(2,1)S(1)} %bitcast.7, ...), custom_call_target="tpu_custom_call" | custom-call | flops 200000000 | bytes 2097152 | tf_op jit(solution)/shard_map/pallas_call | solution.py:270
  56.8 0.0 copy-start
  56.8 1.7 %collective-permute-done.2.refs_1_ = bf16[2,264,512]{2,1,0:T(8,128)(2,1)} collective-permute-done((bf16[2,264,512]{2,1,0:T(8,128)(2,1)}, bf16[2,264,512]{2,1,0:T(8,128)(2,1)}, u32[]{:S(2)}, u32[]{:S(2)}) %collective-permute-start.2) | collective-permute-done | bytes 540704 | tf_op jit(solution)/shard_map/ppermute | solution.py:245
  58.6 3.0 %shard_map.30 = (f32[2,136,512]{2,1,0:T(8,128)S(1)}, f32[2,136,512]{2,1,0:T(8,128)S(1)}) custom-call(s32[2]{0:T(128)S(1)} %compare_select_fusion.refs_0_, bf16[2,264,512]{2,1,0:T(8,128)(2,1)} %collective-permute-done.2.refs_1_, bf16[2,264,512]{2,1,0:T(8,128)(2,1)} %collective-permute-done.6.refs_2_, ...), custom_call_target="tpu_custom_call" | custom-call | flops 200000000 | bytes 2097152 | tf_op jit(solution)/shard_map/pallas_call | solution.py:270
  61.6 1.9 %collective-permute-start.11 = (f32[2,136,512]{2,1,0:T(8,128)S(1)}, f32[2,136,512]{2,1,0:T(8,128)S(1)}, u32[]{:S(2)}, u32[]{:S(2)}) collective-permute-start(f32[2,136,512]{2,1,0:T(8,128)S(1)} %get-tuple-element.16), channel_id=1, source_target_pairs={{0,1},{1,0},{2,3},{3,2},{4,5},{5,4},{6,7},{7,6},{8,9},{9,8},{10,11... | collective-permute-start | bytes 1671176 | tf_op jit(solution)/shard_map/ppermute | solution.py:303
  63.5 1.9 %collective-permute-done.11.received = f32[2,136,512]{2,1,0:T(8,128)S(1)} collective-permute-done((f32[2,136,512]{2,1,0:T(8,128)S(1)}, f32[2,136,512]{2,1,0:T(8,128)S(1)}, u32[]{:S(2)}, u32[]{:S(2)}) %collective-permute-start.11) | collective-permute-done | bytes 557088 | tf_op jit(solution)/shard_map/ppermute | solution.py:303
  65.4 1.0 %shard_map.31 = f32[2,128,512]{2,1,0:T(8,128)} custom-call(f32[2,128,512]{2,1,0:T(8,128)S(1)} %copy-done, f32[2,136,512]{2,1,0:T(8,128)S(1)} %get-tuple-element.15.sums, f32[2,136,512]{2,1,0:T(8,128)S(1)} %collective-permute-done.11.received), custom_call_target="tpu_custom_call" | custom-call | flops 1048576 | bytes 2097152 | tf_op jit(solution)/shard_map/pallas_call | solution.py:304
  (8 shorter events, 0.1 us)
Async XLA Ops:
  2.0 10.5 %collective-permute-start.3 = (bf16[264,512]{1,0:T(8,128)(2,1)S(1)}, bf16[264,512]{1,0:T(8,128)(2,1)S(1)}, u32[]{:S(2)}, u32[]{:S(2)}) collective-permute-start(bf16[264,512]{1,0:T(8,128)(2,1)S(1)} %get-tuple-element.18.refs_1_), channel_id=1, source_target_pairs={{0,2},{1,9},{2,0},{3,11},{4,6},{5,13},{6,4},{7,15},{8,10},{9,1},{1... | collective-permute-start | bytes 811016 | tf_op jit(solution)/shard_map/ppermute | solution.py:245
  6.1 8.4 %collective-permute-start.4 = (bf16[264,512]{1,0:T(8,128)(2,1)S(1)}, bf16[264,512]{1,0:T(8,128)(2,1)S(1)}, u32[]{:S(2)}, u32[]{:S(2)}) collective-permute-start(bf16[264,512]{1,0:T(8,128)(2,1)S(1)} %get-tuple-element.18.refs_1_), channel_id=1, source_target_pairs={{0,6},{1,25},{2,4},{3,27},{4,2},{5,29},{6,0},{7,31},{8,14},{9,17},... | collective-permute-start | bytes 811016 | tf_op jit(solution)/shard_map/ppermute | solution.py:245
  9.9 8.7 %collective-permute-start = (bf16[264,512]{1,0:T(8,128)(2,1)S(1)}, bf16[264,512]{1,0:T(8,128)(2,1)S(1)}, u32[]{:S(2)}, u32[]{:S(2)}) collective-permute-start(bf16[264,512]{1,0:T(8,128)(2,1)S(1)} %get-tuple-element.18.refs_1_), channel_id=1, source_target_pairs={{0,4},{1,17},{2,6},{3,19},{4,0},{5,21},{6,2},{7,23},{8,12},{9,25},... | collective-permute-start | bytes 811016 | tf_op jit(solution)/shard_map/ppermute | solution.py:245
  14.6 30.1 %collective-permute-start.5 = (bf16[2,264,512]{2,1,0:T(8,128)(2,1)S(1)}, bf16[2,264,512]{2,1,0:T(8,128)(2,1)}, u32[]{:S(2)}, u32[]{:S(2)}) collective-permute-start(bf16[2,264,512]{2,1,0:T(8,128)(2,1)S(1)} %pad_maximum_fusion.1.refs_4_), channel_id=1, source_target_pairs={{0,8},{1,3},{2,10},{3,1},{4,12},{5,7},{6,14},{7,5},{8,0},{9,11},{1... | collective-permute-start | bytes 1622024 | tf_op jit(solution)/shard_map/ppermute | solution.py:245
  18.7 29.5 %collective-permute-start.1 = (bf16[2,264,512]{2,1,0:T(8,128)(2,1)S(1)}, bf16[2,264,512]{2,1,0:T(8,128)(2,1)}, u32[]{:S(2)}, u32[]{:S(2)}) collective-permute-start(bf16[2,264,512]{2,1,0:T(8,128)(2,1)S(1)} %pad_maximum_fusion.refs_3_), channel_id=1, source_target_pairs={{0,24},{1,7},{2,26},{3,5},{4,28},{5,3},{6,30},{7,1},{8,16},{9,15},... | collective-permute-start | bytes 1622024 | tf_op jit(solution)/shard_map/ppermute | solution.py:245
  23.1 13.7 %collective-permute-start.7 = (bf16[264,512]{1,0:T(8,128)(2,1)S(1)}, bf16[264,512]{1,0:T(8,128)(2,1)S(1)}, u32[]{:S(2)}, u32[]{:S(2)}) collective-permute-start(bf16[264,512]{1,0:T(8,128)(2,1)S(1)} %get-tuple-element.18.refs_1_), channel_id=1, source_target_pairs={{0,1},{1,0},{2,3},{3,2},{4,5},{5,4},{6,7},{7,6},{8,9},{9,8},{10,11... | collective-permute-start | bytes 811016 | tf_op jit(solution)/shard_map/ppermute | solution.py:251
  29.6 24.9 %collective-permute-start.10 = (bf16[2,264,512]{2,1,0:T(8,128)(2,1)S(1)}, bf16[2,264,512]{2,1,0:T(8,128)(2,1)S(1)}, u32[]{:S(2)}, u32[]{:S(2)}) collective-permute-start(bf16[2,264,512]{2,1,0:T(8,128)(2,1)S(1)} %pad_maximum_fusion.1.refs_4_), channel_id=1, source_target_pairs={{0,24},{1,7},{2,26},{3,5},{4,28},{5,3},{6,30},{7,1},{8,16},{9,15},... | collective-permute-start | bytes 1622024 | tf_op jit(solution)/shard_map/ppermute | solution.py:245
  34.3 20.2 %collective-permute-start.9 = (bf16[2,264,512]{2,1,0:T(8,128)(2,1)S(1)}, bf16[2,264,512]{2,1,0:T(8,128)(2,1)S(1)}, u32[]{:S(2)}, u32[]{:S(2)}) collective-permute-start(bf16[2,264,512]{2,1,0:T(8,128)(2,1)S(1)} %pad_maximum_fusion.refs_3_), channel_id=1, source_target_pairs={{0,8},{1,3},{2,10},{3,1},{4,12},{5,7},{6,14},{7,5},{8,0},{9,11},{1... | collective-permute-start | bytes 1622024 | tf_op jit(solution)/shard_map/ppermute | solution.py:245
  37.6 16.8 %collective-permute-start.8 = (bf16[528,512]{1,0:T(8,128)(2,1)}, bf16[528,512]{1,0:T(8,128)(2,1)S(1)}, u32[]{:S(2)}, u32[]{:S(2)}) collective-permute-start(bf16[528,512]{1,0:T(8,128)(2,1)} %pad_maximum_fusion.2), channel_id=1, source_target_pairs={{0,32},{1,481},{2,34},{3,483},{4,36},{5,485},{6,38},{7,487},{8,40}... | collective-permute-start | bytes 1622024 | tf_op jit(solution)/shard_map/ppermute | solution.py:258
  44.6 12.2 %collective-permute-start.6 = (bf16[2,264,512]{2,1,0:T(8,128)(2,1)}, bf16[2,264,512]{2,1,0:T(8,128)(2,1)}, u32[]{:S(2)}, u32[]{:S(2)}) collective-permute-start(bf16[2,264,512]{2,1,0:T(8,128)(2,1)} %collective-permute-done.5.refs_6_), channel_id=1, source_target_pairs={{0,24},{1,7},{2,26},{3,5},{4,28},{5,3},{6,30},{7,1},{8,16},{9,15},... | collective-permute-start | bytes 1622024 | tf_op jit(solution)/shard_map/ppermute | solution.py:245
  48.2 10.4 %collective-permute-start.2 = (bf16[2,264,512]{2,1,0:T(8,128)(2,1)}, bf16[2,264,512]{2,1,0:T(8,128)(2,1)}, u32[]{:S(2)}, u32[]{:S(2)}) collective-permute-start(bf16[2,264,512]{2,1,0:T(8,128)(2,1)} %collective-permute-done.1.refs_5_), channel_id=1, source_target_pairs={{0,8},{1,3},{2,10},{3,1},{4,12},{5,7},{6,14},{7,5},{8,0},{9,11},{1... | collective-permute-start | bytes 1622024 | tf_op jit(solution)/shard_map/ppermute | solution.py:245
  56.8 8.6 %copy-start = (f32[2,128,512]{2,1,0:T(8,128)S(1)}, f32[2,128,512]{2,1,0:T(8,128)}, u32[]{:S(2)}) copy-start(f32[2,128,512]{2,1,0:T(8,128)} %rows.1) | copy-start | bytes 1572868
  61.6 3.9 %collective-permute-start.11 = (f32[2,136,512]{2,1,0:T(8,128)S(1)}, f32[2,136,512]{2,1,0:T(8,128)S(1)}, u32[]{:S(2)}, u32[]{:S(2)}) collective-permute-start(f32[2,136,512]{2,1,0:T(8,128)S(1)} %get-tuple-element.16), channel_id=1, source_target_pairs={{0,1},{1,0},{2,3},{3,2},{4,5},{5,4},{6,7},{7,6},{8,9},{9,8},{10,11... | collective-permute-start | bytes 1671176 | tf_op jit(solution)/shard_map/ppermute | solution.py:303
